TPU v7x, 128 devices: a whole 4x4x4 slice. The times are simulated.
128 devices in a mesh: dp: 2 (over x_hi), pipe: 2 (over core), expert: 32 (over z, y, x_lo).
Axes of the slice: x: 4 (x_hi: 2, x_lo: 2; x = x_hi * 2 + x_lo), y: 4, z: 4, core: 2. Of those that a mesh axis runs over, the one named last changes fastest.
Arguments:
- inputs: bfloat16 [4, 2048, 1024], P(None, ('dp', 'expert')), may hold values from -6 to 6
- cotangent: bfloat16 [4, 2048, 1024], P(None, ('dp', 'expert')), may hold values from -0.29882812 to 0.29882812
- norm_gain: float32 [2, 1024], P('pipe'), may hold values from 0.5 to 1.5
- w_router: bfloat16 [2, 1024, 32], P('pipe'), may hold values from -0.1875 to 0.1875
- w_gate: bfloat16 [2, 32, 1024, 512], P('pipe', 'expert'), may hold values from -0.1875 to 0.1875
- w_up: bfloat16 [2, 32, 1024, 512], P('pipe', 'expert'), may hold values from -0.1875 to 0.1875
- w_down: bfloat16 [2, 32, 512, 1024], P('pipe', 'expert'), may hold values from -0.25 to 0.25
- routes: int32 [2, 4, 2048, 8], P('pipe', None, ('dp', 'expert')), may hold values from 0 to 31, all different within a row; in each aligned block of 32 rows (0 to 31, 32 to 63, ..., all dimensions but the last counted through in order) at most 10 rows name the same one
Outputs:
- grad_gate: bfloat16 [2, 32, 1024, 512], P('pipe', 'expert', 'dp')
- grad_up: bfloat16 [2, 32, 1024, 512], P('pipe', 'expert', 'dp')
- grad_down: bfloat16 [2, 32, 512, 1024], P('pipe', 'expert', None, 'dp')
- grad_router: float32 [2, 1024, 32], P('pipe')
- grad_gain: float32 [2, 1024], P('pipe')
Inputs may be any that keep to these rules, and one draw needn't show every extreme that they name: `routes`: the experts of a token differ. Among the 32 tokens of one device in one layer and micro-batch, no expert is picked by more than 10 tokens, and some expert is picked by exactly 10 in some of them.
All inputs are finite; a program needn't handle non-finite values.
Results may differ from a plain program's by a relative error of at most 0.012.
Values may be sent and summed in bfloat16 or wider, within the bound.
No kernel may reach another device: no remote copies, remote signals or barrier semaphores. Data moves between devices by JAX's collectives and lax.ppermute only.
A program may use at most 128 MiB of HBM per device.

v0:
```python
import jax
import jax.numpy as jnp
import numpy as np
from jax import lax
from jax.experimental import pallas as pl
from jax.experimental.pallas import tpu as pltpu
from jax.sharding import PartitionSpec as P

EPS = 1e-05
BF = jnp.bfloat16
F32 = jnp.float32

ROWS = 32
CAP = 10
HALF = 2
TOK = ROWS * HALF
EXP = 32
USED = CAP * HALF
SLOT = 24
ALL = EXP * SLOT
LANE = 128


class Tables:
    def __init__(self, n):
        self.n, self.rows, self.made = n, n * SLOT, {}

    def get(self, name, make):
        if name not in self.made:
            self.made[name] = make()
        return self.made[name]

    def place_of(self, shape, axis):
        s = lax.broadcasted_iota(jnp.int32, shape, axis).astype(F32)
        expert = jnp.floor((s + 0.5) * (1.0 / SLOT))
        return expert, s - SLOT * expert

    def flags(self, test):
        return jnp.where(test, 1.0, 0.0)

    @property
    def expand(self):
        def make():
            shape = (self.n, self.rows)
            expert, slot = self.place_of(shape, 1)
            return self.flags(expert == lax.broadcasted_iota(jnp.int32, shape, 0).astype(F32))

        return self.get("expand", make)

    @property
    def expand_t(self):
        def make():
            shape = (self.rows, self.n)
            expert, slot = self.place_of(shape, 0)
            return self.flags(expert == lax.broadcasted_iota(jnp.int32, shape, 1).astype(F32))

        return self.get("expand_t", make)

    @property
    def slot_row(self):
        return self.get("slot_row", lambda: self.place_of((1, self.rows), 1)[1])

    @property
    def slot_column(self):
        return self.get("slot_column", lambda: self.place_of((self.rows, 1), 0)[1])

    @property
    def place(self):
        def make():
            shape = (self.rows, LANE)
            slot = self.place_of(shape, 0)[1]
            lane = lax.broadcasted_iota(jnp.int32, shape, 1).astype(F32)
            return self.flags((slot == lane) & (slot < USED))

        return self.get("place", make)

    def extra(self, i):
        return self.get(("extra", i), lambda: jnp.where(self.slot_row == USED + i, self.expand, 0.0).astype(BF))

    def extra_t(self, i):
        return self.get(("extra_t", i), lambda: jnp.where(self.slot_column == USED + i, self.expand_t, 0.0).astype(BF))


def dot(a, b):
    return lax.dot_general(a, b, (((1,), (0,)), ((), ())), preferred_element_type=F32)


def dot_t0(a, b):
    return lax.dot_general(a, b, (((0,), (0,)), ((), ())), preferred_element_type=F32)


def dot_t1(a, b):
    return lax.dot_general(a, b, (((1,), (1,)), ((), ())), preferred_element_type=F32)


def split2(v):
    hi = v.astype(BF)
    return hi, (v - hi.astype(F32)).astype(BF)


def split3(v):
    hi = v.astype(BF)
    rest = v - hi.astype(F32)
    mid = rest.astype(BF)
    return hi, mid, (rest - mid.astype(F32)).astype(BF)


def slots_of(picks, c):
    columns = lax.broadcasted_iota(jnp.int32, (TOK, EXP), 1)
    mask = jnp.zeros((TOK, EXP), F32)
    for k in range(picks.shape[1]):
        mask = mask + jnp.where(picks[:, k : k + 1] == columns, 1.0, 0.0)
    row = lax.broadcasted_iota(jnp.int32, (TOK, TOK), 0)
    column = lax.broadcasted_iota(jnp.int32, (TOK, TOK), 1)
    earlier = jnp.where((column < row) & ((row < ROWS) | (column >= ROWS)), 1.0, 0.0).astype(BF)
    start = jnp.where(lax.broadcasted_iota(jnp.int32, (TOK, EXP), 0) < ROWS, 0.0, 1.0 * CAP)
    slot = mask * (dot(earlier, mask.astype(BF)) + start + 1.0) - 1.0
    table = dot(slot.astype(BF), c.expand.astype(BF)) == c.slot_row
    return mask, table


def one(table):
    return jnp.where(table, 1.0, 0.0).astype(BF)


def norm(tokens, gain):
    values = tokens.astype(F32)
    scale = lax.rsqrt(jnp.mean(values * values, axis=-1, keepdims=True) + EPS)
    return (values * scale * gain).astype(BF), scale, values


def mix(normed, router, mask):
    logits = dot(normed, router)
    expo = jnp.where(mask > 0.0, jnp.exp(jnp.where(mask > 0.0, logits, 0.0)), 0.0)
    return expo / jnp.sum(expo, axis=-1, keepdims=True)


def weighted(table, parts, c):
    return [jnp.where(table, dot(v, c.expand.astype(BF)), 0.0) for v in parts]


def small_rows(masked, c):
    row = jnp.sum(masked, axis=0, keepdims=True)
    return dot((c.expand * row).astype(BF), c.place.astype(BF))


def small_columns(column, c):
    return dot(c.expand.astype(BF), (column.astype(F32) * c.place).astype(BF))


def spread_rows(smalls, c):
    total = None
    for i, v in enumerate(smalls):
        part = dot(c.extra_t(i), v.astype(BF))
        total = part if total is None else total + part
    return total


def column_of(first, index, c):
    wide = dot(c.expand_t.astype(BF), dot(c.extra(index), first).astype(BF))
    return jnp.sum(wide * c.place, axis=1, keepdims=True)


def with_small(rows, smalls, c):
    first = (rows[:, :LANE] + spread_rows(smalls, c)).astype(BF)
    return first, rows[:, LANE:].astype(BF)


def params(limit=40):
    return pltpu.CompilerParams(vmem_limit_bytes=limit << 20)


def cost(flops, arrays):
    size = sum(int(np.prod(a.shape)) * jnp.dtype(a.dtype).itemsize for a in arrays)
    return pl.CostEstimate(flops=flops, bytes_accessed=size, transcendentals=0)


def run(body, name, outs, args, flops):
    n = len(args)

    def kernel(*refs):
        body(Tables(EXP), refs[:n], refs[n:])

    out_shape = [jax.ShapeDtypeStruct(s, d) for s, d in outs]
    return pl.pallas_call(
        kernel,
        out_shape=out_shape,
        in_specs=[pl.BlockSpec(memory_space=pltpu.VMEM)] * n,
        out_specs=[pl.BlockSpec(memory_space=pltpu.VMEM)] * len(outs),
        name=name,
        cost_estimate=cost(flops, list(args) + out_shape),
        compiler_params=params(),
    )(*args)


PART = 16


def whole(a):
    return pl.BlockSpec(a.shape, lambda i: (0,) * len(a.shape))


def rows_block(width):
    return pl.BlockSpec((PART * SLOT, width), lambda i: (i, 0))


def forward_expert(recv, gate_mat, up_mat, down_mat, name):
    width, inner = gate_mat.shape

    def kernel(x, wg, wu, wd, out, fa, fb, hid):
        rows = x[...]
        gate = dot(rows, wg[...])
        up = dot(rows, wu[...])
        sig = jax.nn.sigmoid(gate)
        act = gate * sig
        hidden = (act * up).astype(BF)
        out[...] = dot(hidden, wd[...]).astype(BF)
        hid[...] = hidden
        fb[...] = act
        fa[...] = up * sig * (1.0 + gate * (1.0 - sig))

    out_shape = [
        jax.ShapeDtypeStruct((ALL, width), BF),
        jax.ShapeDtypeStruct((ALL, inner), F32),
        jax.ShapeDtypeStruct((ALL, inner), F32),
        jax.ShapeDtypeStruct((ALL, inner), BF),
    ]
    args = [recv, gate_mat, up_mat, down_mat]
    return pl.pallas_call(
        kernel,
        grid=(EXP // PART,),
        out_shape=out_shape,
        in_specs=[rows_block(width), whole(gate_mat), whole(up_mat), whole(down_mat)],
        out_specs=[rows_block(width), rows_block(inner), rows_block(inner), rows_block(inner)],
        name=name,
        cost_estimate=cost(6 * ALL * width * inner, args + out_shape),
        compiler_params=params(),
    )(*args)


def backward_expert(recv, grads, out, fa, fb, gate_mat, up_mat, down_mat):
    width, inner = gate_mat.shape

    def kernel(x, g, o, fa, fb, wg, wu, wd, send, scaled_out, gate_out, up_out):
        c = Tables(PART)
        first = x[...]
        weight = column_of(first, 0, c) + column_of(first, 1, c)
        grad = g[...].astype(F32)
        weight_grad = jnp.sum(grad * o[...].astype(F32), axis=1, keepdims=True)
        scaled = (weight * grad).astype(BF)
        scaled_out[...] = scaled
        grad_hidden = dot_t1(scaled, wd[...])
        gate_back = (grad_hidden * fa[...]).astype(BF)
        up_back = (grad_hidden * fb[...]).astype(BF)
        gate_out[...] = gate_back
        up_out[...] = up_back
        back = dot_t1(gate_back, wg[...]) + dot_t1(up_back, wu[...])
        smalls = [small_columns(part, c) for part in split3(weight_grad)]
        send[:, :LANE], send[:, LANE:] = with_small(back, smalls, c)

    out_shape = [
        jax.ShapeDtypeStruct((ALL, width), BF),
        jax.ShapeDtypeStruct((ALL, width), BF),
        jax.ShapeDtypeStruct((ALL, inner), BF),
        jax.ShapeDtypeStruct((ALL, inner), BF),
    ]
    args = [recv, grads, out, fa, fb, gate_mat, up_mat, down_mat]
    return pl.pallas_call(
        kernel,
        grid=(EXP // PART,),
        out_shape=out_shape,
        in_specs=[rows_block(LANE), rows_block(width), rows_block(width), rows_block(inner), rows_block(inner)]
        + [whole(gate_mat), whole(up_mat), whole(down_mat)],
        out_specs=[rows_block(width), rows_block(width), rows_block(inner), rows_block(inner)],
        name="backward1",
        cost_estimate=cost(6 * ALL * width * inner, args + out_shape),
        compiler_params=params(),
    )(*args)


def weight_blocks(at, near, gate_back, up_back, left, scaled, hidden, name):
    width, inner = left.shape[1], hidden.shape[1]
    half, quarter = width // 2, width // 4

    def kernel(at, gb, ub, x, sc, hid, out):
        step = pl.program_id(0)
        pipe, data = at[0], at[1]
        which = jnp.where(step == 0, 1 - pipe, pipe)
        group = data if near else 1 - data
        rows = x[:, pl.ds(pl.multiple_of(group * half + which * quarter, quarter), quarter)]
        out[0, 0:quarter, :] = dot_t0(rows, gb[...]).astype(BF)
        out[0, quarter : 2 * quarter, :] = dot_t0(rows, ub[...]).astype(BF)
        low = hid[:, pl.ds(pl.multiple_of(which * quarter, quarter), quarter)]
        wide = sc[:, pl.ds(pl.multiple_of(group * half, half), half)]
        out[0, 2 * quarter :, :] = dot_t0(low, wide).astype(BF)

    out_shape = jax.ShapeDtypeStruct((2, 3 * quarter, half), BF)
    args = [gate_back, up_back, left, scaled, hidden]
    return pl.pallas_call(
        kernel,
        grid=(2,),
        out_shape=out_shape,
        in_specs=[pl.BlockSpec(memory_space=pltpu.SMEM)] + [whole(v) for v in args],
        out_specs=pl.BlockSpec((1, 3 * quarter, half), lambda i: (i, 0, 0)),
        name=name,
        cost_estimate=cost(3 * ALL * width * inner, args + [out_shape]),
        compiler_params=params(),
    )(at, *args)


def backward_first(recv, fa, fb, down_mat):
    inner = down_mat.shape[0]
    width = down_mat.shape[1]

    def kernel(x, fa, fb, wd, gate_out, up_out):
        grad_hidden = dot_t1(x[...], wd[...])
        gate_out[...] = (grad_hidden * fa[...]).astype(BF)
        up_out[...] = (grad_hidden * fb[...]).astype(BF)

    out_shape = [jax.ShapeDtypeStruct((ALL, inner), BF)] * 2
    args = [recv, fa, fb, down_mat]
    return pl.pallas_call(
        kernel,
        grid=(EXP // PART,),
        out_shape=out_shape,
        in_specs=[rows_block(width), rows_block(inner), rows_block(inner), whole(down_mat)],
        out_specs=[rows_block(inner), rows_block(inner)],
        name="backward0",
        cost_estimate=cost(2 * ALL * width * inner, args + out_shape),
        compiler_params=params(),
    )(*args)


def rest(at, recv0, recv1, recv2, gate_back, up_back, gate_mat, up_mat, gain, gains):
    width, inner = gate_mat.shape
    steps = EXP // PART

    def kernel(at, x0, x1, x2, gb, ub, wg, wu, gain, gains, out, total):
        step = pl.program_id(0)
        c = Tables(PART)

        @pl.when(step == 0)
        def _():
            total[...] = jnp.zeros_like(total)

        first = x2[...]
        back = (dot_t1(gb[...], wg[...]) + dot_t1(ub[...], wu[...])).astype(BF).astype(F32)
        rows0 = x0[...].astype(F32)
        total[0:1, :] += jnp.sum(rows0 * column_of(first, 0, c), axis=0, keepdims=True)
        total[1:2, :] += jnp.sum(rows0 * back, axis=0, keepdims=True)
        total[2:3, :] += jnp.sum(x1[...].astype(F32) * column_of(first, 1, c), axis=0, keepdims=True)

        @pl.when(step == steps - 1)
        def _():
            gain0 = total[1:2, :] / gain[...] + gains[1:2, :]
            gain1 = gains[0:1, :]
            mine = at[0] == 0
            column0, column1 = total[0:1, :], total[2:3, :]
            out[0:1, :] = jnp.where(mine, column0, column1)
            out[1:2, :] = jnp.where(mine, gain0, gain1)
            out[2:3, :] = jnp.where(mine, column1, column0)
            out[3:4, :] = jnp.where(mine, gain1, gain0)

    out_shape = jax.ShapeDtypeStruct((4, width), F32)
    args = [recv0, recv1, recv2, gate_back, up_back, gate_mat, up_mat, gain, gains]
    return pl.pallas_call(
        kernel,
        grid=(steps,),
        out_shape=out_shape,
        in_specs=[pl.BlockSpec(memory_space=pltpu.SMEM), rows_block(width), rows_block(width), rows_block(LANE)]
        + [rows_block(inner), rows_block(inner), whole(gate_mat), whole(up_mat), whole(gain), whole(gains)],
        out_specs=whole(out_shape),
        scratch_shapes=[pltpu.VMEM((8, width), F32)],
        name="rest",
        cost_estimate=cost(4 * ALL * width * inner, args),
        compiler_params=params(),
    )(at, *args)


def start_body(c, ins, outs):
    tokens, picks, gain, router = ins
    send, weights = outs
    mask, table = slots_of(picks[...], c)
    normed, scale, values = norm(tokens[...], gain[...])
    weights[...] = mix(normed, router[...], mask)
    send[...] = dot_t0(one(table), normed).astype(BF)


def cotangent_body(c, ins, outs):
    grad, picks = ins
    (send,) = outs
    mask, table = slots_of(picks[...], c)
    send[...] = dot_t0(one(table), grad[...]).astype(BF)


def middle_body(c, ins, outs):
    tokens, picks0, weights0, returned, picks1, gain1, router1 = ins
    mixed_out, send, weights1 = outs
    mask0, table0 = slots_of(picks0[...], c)
    hi, lo = weighted(table0, split2(weights0[...]), c)
    back = returned[...]
    mixed = tokens[...].astype(F32) + dot(hi.astype(BF), back) + dot(lo.astype(BF), back)
    mixed = mixed.astype(BF)
    mixed_out[...] = mixed
    mask1, table1 = slots_of(picks1[...], c)
    normed, scale, values = norm(mixed, gain1[...])
    weights = mix(normed, router1[...], mask1)
    weights1[...] = weights
    rows = dot_t0(one(table1), normed)
    smalls = [small_rows(v, c) for v in weighted(table1, split2(weights), c)]
    send[:, :LANE], send[:, LANE:] = with_small(rows, smalls, c)


def turn_body(c, ins, outs):
    (tokens1, picks1, weights1, returned1, gain1, router1, grad, tokens0, picks0, weights0, returned0, gain0, router0) = ins
    send, gains = outs
    mask1, table1 = slots_of(picks1[...], c)
    back1 = returned1[...]
    pick1 = one(table1)
    expert_part = dot(pick1, back1)
    w1 = weights1[...]
    wg1 = jnp.zeros((TOK, EXP), F32)
    for i in range(3):
        column = column_of(back1[:, :LANE], i, c)
        wg1 = wg1 + dot(pick1, (column * c.expand_t).astype(BF))
    lg1 = (w1 * (wg1 - jnp.sum(w1 * wg1, axis=-1, keepdims=True))).astype(BF)
    normed1, scale1, values1 = norm(tokens1[...], gain1[...])
    normed_grad1 = dot_t1(lg1, router1[...]) + expert_part
    gains[0:1, :] = jnp.sum(normed_grad1 * values1 * scale1, axis=0, keepdims=True)
    q = normed_grad1 * gain1[...]
    grad_f = grad[...].astype(F32)
    g0 = (
        grad_f + scale1 * q - scale1 * scale1 * scale1 * values1 * jnp.mean(q * values1, axis=-1, keepdims=True)
    ).astype(BF)
    mask0, table0 = slots_of(picks0[...], c)
    w0 = weights0[...]
    met = jnp.where(table0, dot_t1(g0, returned0[...]), 0.0)
    wg0 = jnp.zeros((TOK, EXP), F32)
    for part in split3(met):
        wg0 = wg0 + dot(part, c.expand_t.astype(BF))
    lg0 = (w0 * (wg0 - jnp.sum(w0 * wg0, axis=-1, keepdims=True))).astype(BF)
    normed0, scale0, values0 = norm(tokens0[...], gain0[...])
    gains[1:2, :] = jnp.sum(dot_t1(lg0, router0[...]) * values0 * scale0, axis=0, keepdims=True)
    hi, lo = weighted(table0, split2(w0), c)
    rows = dot_t0(hi.astype(BF), g0) + dot_t0(lo.astype(BF), g0)
    smalls = [small_rows(weighted(table0, [lg0], c)[0], c), small_rows(weighted(table1, [lg1], c)[0], c)]
    send[:, :LANE], send[:, LANE:] = with_small(rows, smalls, c)


def exchanged(rows):
    return lax.all_to_all(rows, "expert", split_axis=0, concat_axis=0, tiled=True)


def swapped(value):
    return lax.ppermute(value, "pipe", [(0, 1), (1, 0)])


def shards(inputs, cotangent, norm_gain, w_router, w_gate, w_up, w_down, routes):
    pipe = lax.axis_index("pipe")
    data = lax.axis_index("dp")
    at = jnp.stack([pipe, data]).astype(jnp.int32)
    width = inputs.shape[-1]
    first = pipe == 0

    def own_part(v):
        return lax.dynamic_slice_in_dim(v, pipe * HALF, HALF, 0).reshape(TOK, -1)

    def other_part(v):
        return lax.dynamic_slice_in_dim(v, (1 - pipe) * HALF, HALF, 0).reshape(TOK, -1)

    def both(own, other):
        return jnp.where(first, own, other), jnp.where(first, other, own)

    picks0, picks1 = both(own_part(routes[0]), swapped(other_part(routes[0])))
    gain0, gain1 = both(norm_gain, swapped(norm_gain))
    router0, router1 = both(w_router[0], swapped(w_router[0]))
    tokens0 = own_part(inputs)
    grad1 = own_part(cotangent)

    rows_shape = ((ALL, width), BF)
    send0, weights0 = run(
        start_body, "start", [rows_shape, ((TOK, EXP), F32)], [tokens0, picks0, gain0, router0], 100_000_000
    )
    recv0 = exchanged(send0)
    mats = [both(w[0, 0], swapped(w[0, 0])) for w in (w_gate, w_up, w_down)]
    (gate0, gate1), (up0, up1), (down0, down1) = lax.optimization_barrier(mats)
    (send_g,) = run(cotangent_body, "cotangent", [rows_shape], [grad1, picks1], 100_000_000)
    grad_rows = exchanged(send_g)

    out0, fa0, fb0, hidden0 = forward_expert(recv0, gate0, up0, down0, "forward0")
    returned0 = exchanged(out0)

    tokens1, send1, weights1 = run(
        middle_body,
        "middle",
        [((TOK, width), BF), rows_shape, ((TOK, EXP), F32)],
        [tokens0, picks0, weights0, returned0, picks1, gain1, router1],
        300_000_000,
    )
    recv1 = exchanged(send1)

    out1, fa1, fb1, hidden1 = forward_expert(recv1, gate1, up1, down1, "forward1")
    send_b, scaled1, gate_back1, up_back1 = backward_expert(recv1, grad_rows, out1, fa1, fb1, gate1, up1, down1)
    returned1 = exchanged(send_b)

    def over_groups(args, name):
        far = weight_blocks(at, False, *args, name + "_far")
        far = (far[1].astype(F32) + swapped(far[0]).astype(F32)).astype(BF)
        got = lax.ppermute(far, "dp", [(0, 1), (1, 0)])
        near = weight_blocks(at, True, *args, name + "_near")
        near = near[1].astype(F32) + swapped(near[0]).astype(F32)
        return (near + got.astype(F32)).astype(BF)

    summed1 = over_groups([gate_back1, up_back1, recv1, scaled1, hidden1], "grads1")

    send2, gains = run(
        turn_body,
        "turn",
        [rows_shape, ((2, width), F32)],
        [tokens1, picks1, weights1, returned1, gain1, router1, grad1, tokens0, picks0, weights0, returned0, gain0, router0],
        600_000_000,
    )
    recv2 = exchanged(send2)
    gate_back0, up_back0 = backward_first(recv2, fa0, fb0, down0)
    summed0 = over_groups([gate_back0, up_back0, recv0, recv2, hidden0], "grads0")

    small = rest(at, recv0, recv1, recv2, gate_back0, up_back0, gate0, up0, gain0, gains)
    mine = small[0:2] + swapped(small[2:4])
    group = 2 * EXP
    told = jnp.broadcast_to(mine.reshape(1, 2 * width // LANE, LANE), (group, 2 * width // LANE, LANE))
    heard = lax.all_to_all(told, ("dp", "expert"), split_axis=0, concat_axis=0, tiled=True)
    heard = heard.reshape(2, EXP, 2, width)
    router_sum = (heard[0, :, 0] + heard[1, :, 0]).T
    gain_sum = jnp.sum(heard[:, :, 1], axis=(0, 1))

    mine, theirs = both(summed0, summed1)
    low, high = both(mine, swapped(theirs))
    quarter = low.shape[0] // 3
    outs = [
        jnp.concatenate([low[i * quarter : (i + 1) * quarter], high[i * quarter : (i + 1) * quarter]], axis=0)
        for i in range(3)
    ]
    return (
        outs[0][None, None],
        outs[1][None, None],
        outs[2][None, None],
        router_sum[None],
        gain_sum[None],
    )


def solution(mesh):
    in_specs = (
        P(None, ("dp", "expert"), None),
        P(None, ("dp", "expert"), None),
        P("pipe", None),
        P("pipe", None, None),
        P("pipe", "expert", None, None),
        P("pipe", "expert", None, None),
        P("pipe", "expert", None, None),
        P("pipe", None, ("dp", "expert"), None),
    )
    out_specs = (
        P("pipe", "expert", "dp", None),
        P("pipe", "expert", "dp", None),
        P("pipe", "expert", None, "dp"),
        P("pipe", None, None),
        P("pipe", None),
    )
    return jax.shard_map(shards, mesh=mesh, in_specs=in_specs, out_specs=out_specs, check_vma=False)
```

profile of v0, /device:TPU:0, one launch (start us, length us, event | category | flops | bytes accessed | tf_op | source)
XLA Modules:
  0.0 270.5 jit_solution(6693064364003539496)
XLA Ops:
  6.0 2.2 start.1
  8.8 9.5 %all-to-all-start = ((bf16[32,24,1024]{2,1,0:T(8,128)(2,1)}), bf16[32,24,1024]{2,1,0:T(8,128)(2,1)S(1)}, u32[]{:S(2)}, u32[]{:S(2)}) async-start(bf16[32,24,1024]{2,1,0:T(8,128)(2,1)} %bitcast.6), calls=%async_computation | async-start | bytes 3145728 | tf_op jit(solution)/shard_map/all_to_all | solution.py:451
  18.5 2.8 %broadcast_select_fusion = (bf16[512,1024]{1,0:T(8,128)(2,1)}, bf16[512,1024]{1,0:T(8,128)(2,1)}) fusion(bf16[512,1024]{1,0:T(8,128)(2,1)} %collective-permute-done.5, pred[]{:T(512)S(6)} %eq.3, bf16[1,1,512,1024]{3,2,1,0:T(8,128)(2,1)S(1)} %copy-done.63), kind=kLoop, calls=%fused_computation.10 | loop fusion | flops 1048576 | bytes 4194305 | tf_op jit(solution)/shard_map/jit(_where)/select_n | solution.py:472
  21.3 2.4 broadcast_select_fusion.2
  23.7 1.6 broadcast_select_fusion.4
  25.4 17.0 %all-to-all-done = bf16[32,24,1024]{2,1,0:T(8,128)(2,1)S(1)} async-done(((bf16[32,24,1024]{2,1,0:T(8,128)(2,1)}), bf16[32,24,1024]{2,1,0:T(8,128)(2,1)S(1)}, u32[]{:S(2)}, u32[]{:S(2)}) %all-to-all-start) | async-done | bytes 1572896 | tf_op jit(solution)/shard_map/all_to_all | solution.py:451
  42.3 1.8 copy-done.15
  45.4 3.1 %forward0.1 = (bf16[768,1024]{1,0:T(8,128)(2,1)S(1)}, f32[768,512]{1,0:T(8,128)S(1)}, f32[768,512]{1,0:T(8,128)S(1)}, bf16[768,512]{1,0:T(8,128)(2,1)S(1)}) custom-call(bf16[768,1024]{1,0:T(8,128)(2,1)S(1)} %bitcast.85, bf16[1024,512]{1,0:T(8,128)(2,1)S(1)} %copy-done.15, bf16[1024,512]{1,0:T(8,128)(2,1)S(1)} %get-tuple-element.35.wu, ...), custom_call_target="tpu_custom_call" | custom-call | flops 2415919104 | bytes 10223616 | tf_op jit(solution)/shard_map/forward0/pallas_call | solution.py:229
  49.6 26.9 %all_to_all.71 = bf16[32,24,1024]{2,1,0:T(8,128)(2,1)S(1)} all-to-all(bf16[32,24,1024]{2,1,0:T(8,128)(2,1)S(1)} %bitcast.99), channel_id=1, replica_groups=mesh['dp'=2,'pipe'=2,'expert'=32] {'expert'}, dimensions={0} | all-to-all | bytes 3145728 | tf_op jit(solution)/shard_map/all_to_all | solution.py:451
  76.6 2.5 middle.1
  81.5 4.1 %all-to-all-start.2 = ((bf16[32,24,1024]{2,1,0:T(8,128)(2,1)}), bf16[32,24,1024]{2,1,0:T(8,128)(2,1)S(1)}, u32[]{:S(2)}, u32[]{:S(2)}) async-start(bf16[32,24,1024]{2,1,0:T(8,128)(2,1)} %bitcast.98), calls=%async_computation.2 | async-start | bytes 3145728 | tf_op jit(solution)/shard_map/all_to_all | solution.py:451
  88.7 19.3 %all-to-all-done.2 = bf16[32,24,1024]{2,1,0:T(8,128)(2,1)S(1)} async-done(((bf16[32,24,1024]{2,1,0:T(8,128)(2,1)}), bf16[32,24,1024]{2,1,0:T(8,128)(2,1)S(1)}, u32[]{:S(2)}, u32[]{:S(2)}) %all-to-all-start.2) | async-done | bytes 1572896 | tf_op jit(solution)/shard_map/all_to_all | solution.py:451
  108.0 4.9 %all-to-all-start.3 = ((bf16[32,24,1024]{2,1,0:T(8,128)(2,1)}), bf16[32,24,1024]{2,1,0:T(8,128)(2,1)}, u32[]{:S(2)}, u32[]{:S(2)}) async-start(bf16[32,24,1024]{2,1,0:T(8,128)(2,1)} %bitcast.91), calls=%async_computation.3 | async-start | bytes 3145728 | tf_op jit(solution)/shard_map/all_to_all | solution.py:451
  116.5 3.1 %forward1.1 = (bf16[768,1024]{1,0:T(8,128)(2,1)S(1)}, f32[768,512]{1,0:T(8,128)S(1)}, f32[768,512]{1,0:T(8,128)S(1)}, bf16[768,512]{1,0:T(8,128)(2,1)S(1)}) custom-call(bf16[768,1024]{1,0:T(8,128)(2,1)S(1)} %bitcast.76, bf16[1024,512]{1,0:T(8,128)(2,1)S(1)} %copy-done.23, bf16[1024,512]{1,0:T(8,128)(2,1)S(1)} %copy-done.21, bf16[512,1024]{1,0:T(8,128)(2,1)S(1)} %copy-done.19), custom_call_target="tpu_custom_call" | custom-call | flops 2415919104 | bytes 10223616 | tf_op jit(solution)/shard_map/forward1/pallas_call | solution.py:229
  124.1 10.9 %all-to-all-done.3 = bf16[32,24,1024]{2,1,0:T(8,128)(2,1)} async-done(((bf16[32,24,1024]{2,1,0:T(8,128)(2,1)}), bf16[32,24,1024]{2,1,0:T(8,128)(2,1)}, u32[]{:S(2)}, u32[]{:S(2)}) %all-to-all-start.3) | async-done | bytes 1572896 | tf_op jit(solution)/shard_map/all_to_all | solution.py:451
  141.5 6.0 %backward1.1 = (bf16[768,1024]{1,0:T(8,128)(2,1)S(1)}, bf16[768,1024]{1,0:T(8,128)(2,1)S(1)}, bf16[768,512]{1,0:T(8,128)(2,1)S(1)}, bf16[768,512]{1,0:T(8,128)(2,1)S(1)}) custom-call(bf16[768,1024]{1,0:T(8,128)(2,1)S(1)} %bitcast.77, bf16[768,1024]{1,0:T(8,128)(2,1)} %bitcast.17.g, bf16[768,1024]{1,0:T(8,128)(2,1)S(1)} %copy-done.44, ...), custom_call_target="tpu_custom_call" | custom-call | flops 2415919104 | bytes 15728640 | tf_op jit(solution)/shard_map/backward1/pallas_call | solution.py:268
  147.6 26.9 %all_to_all.72 = bf16[32,24,1024]{2,1,0:T(8,128)(2,1)S(1)} all-to-all(bf16[32,24,1024]{2,1,0:T(8,128)(2,1)S(1)} %bitcast.97), channel_id=1, replica_groups=mesh['dp'=2,'pipe'=2,'expert'=32] {'expert'}, dimensions={0} | all-to-all | bytes 3145728 | tf_op jit(solution)/shard_map/all_to_all | solution.py:451
  174.6 5.2 %turn.1 = (bf16[768,1024]{1,0:T(8,128)(2,1)S(1)}, f32[2,1024]{1,0:T(2,128)S(1)}) custom-call(bf16[64,1024]{1,0:T(8,128)(2,1)S(1)} %copy-done.60, s32[64,8]{1,0:T(8,128)S(1)} %copy-done.52, f32[64,32]{1,0:T(8,128)S(1)} %copy-done.62, bf16[768,1024]{1,0:T(8,128)(2,1)S(1)} %bitcast.92, f32[1,1024]{1,0:T(1,128)S(1)} %get-tuple-element.82.refs_5_.refs_4_, ...), custom_call_target="tpu_custom_call" | custom-call | flops 600000000 | bytes 5279744 | tf_op jit(solution)/shard_map/turn/pallas_call | solution.py:185
  180.9 4.0 %all-to-all-start.5 = ((bf16[32,24,1024]{2,1,0:T(8,128)(2,1)}), bf16[32,24,1024]{2,1,0:T(8,128)(2,1)S(1)}, u32[]{:S(2)}, u32[]{:S(2)}) async-start(bf16[32,24,1024]{2,1,0:T(8,128)(2,1)} %bitcast.96), calls=%async_computation.5 | async-start | bytes 3145728 | tf_op jit(solution)/shard_map/all_to_all | solution.py:451
  185.0 1.4 copy-done.9
  189.8 2.2 grads1_far.1
  193.5 2.2 grads1_near.1
  196.8 10.3 %all-to-all-done.5 = bf16[32,24,1024]{2,1,0:T(8,128)(2,1)S(1)} async-done(((bf16[32,24,1024]{2,1,0:T(8,128)(2,1)}), bf16[32,24,1024]{2,1,0:T(8,128)(2,1)S(1)}, u32[]{:S(2)}, u32[]{:S(2)}) %all-to-all-start.5) | async-done | bytes 1572896 | tf_op jit(solution)/shard_map/all_to_all | solution.py:451
  212.8 2.2 grads0_far.1
  217.4 2.3 fusion
  219.7 2.7 %collective-permute-start.11 = (bf16[768,512]{1,0:T(8,128)(2,1)}, bf16[768,512]{1,0:T(8,128)(2,1)}, u32[]{:S(2)}, u32[]{:S(2)}) collective-permute-start(bf16[768,512]{1,0:T(8,128)(2,1)} %fusion), channel_id=1, source_target_pairs={{0,64},{64,0},{1,65},{65,1},{2,66},{66,2},{3,67},{67,3},{4,68},{68... | collective-permute-start | bytes 2359304 | tf_op jit(solution)/shard_map/ppermute | solution.py:509
  222.4 2.2 grads0_near.1
  227.8 3.8 %rest.1 = f32[4,1024]{1,0:T(4,128)S(1)} custom-call(s32[2]{0:T(128)S(1)} %pad_add_fusion.at, bf16[768,1024]{1,0:T(8,128)(2,1)S(1)} %bitcast.88, bf16[768,1024]{1,0:T(8,128)(2,1)S(1)} %bitcast.80, bf16[768,1024]{1,0:T(8,128)(2,1)S(1)} %bitcast.84, bf16[768,512]{1,0:T(8,128)(2,1)S(1)} %get-tuple-element.51.gb, bf16[768,512]{1,0:T(8,128)(2,1)S(1)} %get-tuple-element.52.ub, ...), custom_call_target="tpu_custom_call" | custom-call | flops 1610612736 | bytes 8400896 | tf_op jit(solution)/shard_map/rest/pallas_call | solution.py:366
  233.8 6.9 %all-to-all-start.6 = ((f32[64,16,128]{2,1,0:T(8,128)}), f32[64,16,128]{2,1,0:T(8,128)}, u32[]{:S(2)}, u32[]{:S(2)}) async-start(f32[64,16,128]{2,1,0:T(8,128)} %broadcast_in_dim.26), calls=%async_computation.6 | async-start | bytes 1048576 | tf_op jit(solution)/shard_map/all_to_all | solution.py:531
  241.9 16.9 %collective-permute-done.8 = bf16[768,512]{1,0:T(8,128)(2,1)} collective-permute-done((bf16[768,512]{1,0:T(8,128)(2,1)}, bf16[768,512]{1,0:T(8,128)(2,1)}, u32[]{:S(2)}, u32[]{:S(2)}) %collective-permute-start.8) | collective-permute-done | bytes 786464 | tf_op jit(solution)/shard_map/ppermute | solution.py:509
  258.8 3.7 %broadcast_select_fusion.8 = (bf16[768,512]{1,0:T(8,128)(2,1)}, bf16[768,512]{1,0:T(8,128)(2,1)S(1)}, bf16[768,512]{1,0:T(8,128)(2,1)S(1)}) fusion(pred[]{:T(512)S(6)} %eq.3, bf16[768,512]{1,0:T(8,128)(2,1)} %collective-permute-done.8, bf16[768,512]{1,0:T(8,128)(2,1)} %collective-permute-done.6, bf16[2,768,512]{2,1,0:T(8,128)(2,1)} %copy-done.7, ...), kind=kLoop, calls=%fused_computation.26 | loop fusion | flops 5111808 | bytes 7077889 | tf_op jit(solution)/shard_map/jit(_where)/select_n | solution.py:472
  262.5 2.2 all-to-all-done.6
  (186 shorter events, 56.1 us)
Async XLA Ops:
  0.6 3.9 %collective-permute-start.1 = (f32[1,1024]{1,0:T(1,128)}, f32[1,1024]{1,0:T(1,128)S(1)}, u32[]{:S(2)}, u32[]{:S(2)}) collective-permute-start(f32[1,1024]{1,0:T(1,128)} %param.10), channel_id=1, source_target_pairs={{0,32},{32,0},{1,33},{33,1},{2,34},{34,2},{3,35},{35,3},{4,36},{36... | collective-permute-start | bytes 12296 | tf_op jit(solution)/shard_map/ppermute | solution.py:455
  1.6 2.3 collective-permute-start
  3.1 2.1 collective-permute-start.2
  3.2 15.3 %collective-permute-start.5 = (bf16[512,1024]{1,0:T(8,128)(2,1)}, bf16[512,1024]{1,0:T(8,128)(2,1)}, u32[]{:S(2)}, u32[]{:S(2)}) collective-permute-start(bf16[512,1024]{1,0:T(8,128)(2,1)} %bitcast.102), channel_id=1, source_target_pairs={{0,32},{32,0},{1,33},{33,1},{2,34},{34,2},{3,35},{35,3},{4,36},{36... | collective-permute-start | bytes 3145736 | tf_op jit(solution)/shard_map/ppermute | solution.py:455
  3.7 17.6 %collective-permute-start.4 = (bf16[1024,512]{1,0:T(8,128)(2,1)}, bf16[1024,512]{1,0:T(8,128)(2,1)}, u32[]{:S(2)}, u32[]{:S(2)}) collective-permute-start(bf16[1024,512]{1,0:T(8,128)(2,1)} %bitcast.103), channel_id=1, source_target_pairs={{0,32},{32,0},{1,33},{33,1},{2,34},{34,2},{3,35},{35,3},{4,36},{36... | collective-permute-start | bytes 3145736 | tf_op jit(solution)/shard_map/ppermute | solution.py:455
  8.8 33.5 %all-to-all-start = ((bf16[32,24,1024]{2,1,0:T(8,128)(2,1)}), bf16[32,24,1024]{2,1,0:T(8,128)(2,1)S(1)}, u32[]{:S(2)}, u32[]{:S(2)}) async-start(bf16[32,24,1024]{2,1,0:T(8,128)(2,1)} %bitcast.6), calls=%async_computation | async-start | bytes 3145728 | tf_op jit(solution)/shard_map/all_to_all | solution.py:451
  18.3 5.4 %collective-permute-start.3 = (bf16[1024,512]{1,0:T(8,128)(2,1)}, bf16[1024,512]{1,0:T(8,128)(2,1)S(1)}, u32[]{:S(2)}, u32[]{:S(2)}) collective-permute-start(bf16[1024,512]{1,0:T(8,128)(2,1)} %bitcast.104), channel_id=1, source_target_pairs={{0,32},{32,0},{1,33},{33,1},{2,34},{34,2},{3,35},{35,3},{4,36},{36... | collective-permute-start | bytes 3145736 | tf_op jit(solution)/shard_map/ppermute | solution.py:455
  49.6 26.9 %copy-start.54 = (s32[64,8]{1,0:T(8,128)S(1)}, s32[64,8]{1,0:T(8,128)}, u32[]{:S(2)}) copy-start(s32[64,8]{1,0:T(8,128)} %copy-done.53) | copy-start | bytes 6148
  81.5 26.5 %all-to-all-start.2 = ((bf16[32,24,1024]{2,1,0:T(8,128)(2,1)}), bf16[32,24,1024]{2,1,0:T(8,128)(2,1)S(1)}, u32[]{:S(2)}, u32[]{:S(2)}) async-start(bf16[32,24,1024]{2,1,0:T(8,128)(2,1)} %bitcast.98), calls=%async_computation.2 | async-start | bytes 3145728 | tf_op jit(solution)/shard_map/all_to_all | solution.py:451
  108.0 27.0 %all-to-all-start.3 = ((bf16[32,24,1024]{2,1,0:T(8,128)(2,1)}), bf16[32,24,1024]{2,1,0:T(8,128)(2,1)}, u32[]{:S(2)}, u32[]{:S(2)}) async-start(bf16[32,24,1024]{2,1,0:T(8,128)(2,1)} %bitcast.91), calls=%async_computation.3 | async-start | bytes 3145728 | tf_op jit(solution)/shard_map/all_to_all | solution.py:451
  147.4 27.0 %copy-start.8 = (bf16[768,1024]{1,0:T(8,128)(2,1)}, bf16[768,1024]{1,0:T(8,128)(2,1)S(1)}, u32[]{:S(2)}) copy-start(bf16[768,1024]{1,0:T(8,128)(2,1)S(1)} %get-tuple-element.56.sc) | copy-start | bytes 4718596
  147.4 27.0 %copy-start.29 = (bf16[768,512]{1,0:T(8,128)(2,1)}, bf16[768,512]{1,0:T(8,128)(2,1)S(1)}, u32[]{:S(2)}) copy-start(bf16[768,512]{1,0:T(8,128)(2,1)S(1)} %get-tuple-element.54.gb) | copy-start | bytes 2359300
  147.5 27.0 %copy-start.31 = (bf16[768,512]{1,0:T(8,128)(2,1)}, bf16[768,512]{1,0:T(8,128)(2,1)S(1)}, u32[]{:S(2)}) copy-start(bf16[768,512]{1,0:T(8,128)(2,1)S(1)} %get-tuple-element.55.ub) | copy-start | bytes 2359300
  147.5 27.0 %copy-start.34 = (bf16[1024,32]{1,0:T(8,128)(2,1)S(1)}, bf16[1024,32]{1,0:T(8,128)(2,1)}, u32[]{:S(2)}) copy-start(bf16[1024,32]{1,0:T(8,128)(2,1)} %copy-done.33) | copy-start | bytes 196612
  147.5 27.0 %copy-start.36 = (bf16[1024,32]{1,0:T(8,128)(2,1)S(1)}, bf16[1024,32]{1,0:T(8,128)(2,1)}, u32[]{:S(2)}) copy-start(bf16[1024,32]{1,0:T(8,128)(2,1)} %get-tuple-element.76.refs_6_.refs_5_) | copy-start | bytes 196612
  147.5 27.0 %copy-start.49 = (bf16[2,32,1024]{2,1,0:T(8,128)(2,1)S(1)}, bf16[2,32,1024]{2,1,0:T(8,128)(2,1)}, u32[]{:S(2)}) copy-start(bf16[2,32,1024]{2,1,0:T(8,128)(2,1)} %copy-done.48) | copy-start | bytes 393220
  147.5 27.0 %copy-start.52 = (s32[64,8]{1,0:T(8,128)S(1)}, s32[64,8]{1,0:T(8,128)}, u32[]{:S(2)}) copy-start(s32[64,8]{1,0:T(8,128)} %get-tuple-element.78.refs_4_.refs_1_) | copy-start | bytes 6148
  147.5 27.0 %copy-start.55 = (s32[64,8]{1,0:T(8,128)S(1)}, s32[64,8]{1,0:T(8,128)}, u32[]{:S(2)}) copy-start(s32[64,8]{1,0:T(8,128)} %copy-done.53) | copy-start | bytes 6148
  147.5 27.0 %copy-start.58 = (f32[64,32]{1,0:T(8,128)S(1)}, f32[64,32]{1,0:T(8,128)}, u32[]{:S(2)}) copy-start(f32[64,32]{1,0:T(8,128)} %copy-done.56) | copy-start | bytes 24580
  147.5 27.0 %copy-start.60 = (bf16[64,1024]{1,0:T(8,128)(2,1)S(1)}, bf16[64,1024]{1,0:T(8,128)(2,1)}, u32[]{:S(2)}) copy-start(bf16[64,1024]{1,0:T(8,128)(2,1)} %copy-done.59) | copy-start | bytes 393220
  147.5 27.0 %copy-start.62 = (f32[64,32]{1,0:T(8,128)S(1)}, f32[64,32]{1,0:T(8,128)}, u32[]{:S(2)}) copy-start(f32[64,32]{1,0:T(8,128)} %copy-done.61) | copy-start | bytes 24580
  180.9 26.2 %all-to-all-start.5 = ((bf16[32,24,1024]{2,1,0:T(8,128)(2,1)}), bf16[32,24,1024]{2,1,0:T(8,128)(2,1)S(1)}, u32[]{:S(2)}, u32[]{:S(2)}) async-start(bf16[32,24,1024]{2,1,0:T(8,128)(2,1)} %bitcast.96), calls=%async_computation.5 | async-start | bytes 3145728 | tf_op jit(solution)/shard_map/all_to_all | solution.py:451
  193.5 23.9 %collective-permute-start.10 = (bf16[768,512]{1,0:T(8,128)(2,1)}, bf16[768,512]{1,0:T(8,128)(2,1)}, u32[]{:S(2)}, u32[]{:S(2)}) collective-permute-start(bf16[768,512]{1,0:T(8,128)(2,1)} %slice_bitcast_fusion), channel_id=1, source_target_pairs={{0,32},{32,0},{1,33},{33,1},{2,34},{34,2},{3,35},{35,3},{4,36},{36... | collective-permute-start | bytes 2359304 | tf_op jit(solution)/shard_map/ppermute | solution.py:455
  215.1 10.8 %collective-permute-start.7 = (bf16[768,512]{1,0:T(8,128)(2,1)S(1)}, bf16[768,512]{1,0:T(8,128)(2,1)S(1)}, u32[]{:S(2)}, u32[]{:S(2)}) collective-permute-start(bf16[768,512]{1,0:T(8,128)(2,1)S(1)} %slice_bitcast_fusion.4), channel_id=1, source_target_pairs={{0,32},{32,0},{1,33},{33,1},{2,34},{34,2},{3,35},{35,3},{4,36},{36... | collective-permute-start | bytes 2359304 | tf_op jit(solution)/shard_map/ppermute | solution.py:455
  217.4 23.4 %collective-permute-start.9 = (bf16[768,512]{1,0:T(8,128)(2,1)}, bf16[768,512]{1,0:T(8,128)(2,1)}, u32[]{:S(2)}, u32[]{:S(2)}) collective-permute-start(bf16[768,512]{1,0:T(8,128)(2,1)} %slice_bitcast_fusion.2), channel_id=1, source_target_pairs={{0,32},{32,0},{1,33},{33,1},{2,34},{34,2},{3,35},{35,3},{4,36},{36... | collective-permute-start | bytes 2359304 | tf_op jit(solution)/shard_map/ppermute | solution.py:455
  219.7 22.2 %collective-permute-start.11 = (bf16[768,512]{1,0:T(8,128)(2,1)}, bf16[768,512]{1,0:T(8,128)(2,1)}, u32[]{:S(2)}, u32[]{:S(2)}) collective-permute-start(bf16[768,512]{1,0:T(8,128)(2,1)} %fusion), channel_id=1, source_target_pairs={{0,64},{64,0},{1,65},{65,1},{2,66},{66,2},{3,67},{67,3},{4,68},{68... | collective-permute-start | bytes 2359304 | tf_op jit(solution)/shard_map/ppermute | solution.py:509
  225.6 16.3 %collective-permute-start.6 = (bf16[768,512]{1,0:T(8,128)(2,1)}, bf16[768,512]{1,0:T(8,128)(2,1)}, u32[]{:S(2)}, u32[]{:S(2)}) collective-permute-start(bf16[768,512]{1,0:T(8,128)(2,1)} %slice_bitcast_fusion.6), channel_id=1, source_target_pairs={{0,32},{32,0},{1,33},{33,1},{2,34},{34,2},{3,35},{35,3},{4,36},{36... | collective-permute-start | bytes 2359304 | tf_op jit(solution)/shard_map/ppermute | solution.py:455
  227.0 31.8 %collective-permute-start.8 = (bf16[768,512]{1,0:T(8,128)(2,1)}, bf16[768,512]{1,0:T(8,128)(2,1)}, u32[]{:S(2)}, u32[]{:S(2)}) collective-permute-start(bf16[768,512]{1,0:T(8,128)(2,1)} %fusion.3), channel_id=1, source_target_pairs={{0,64},{64,0},{1,65},{65,1},{2,66},{66,2},{3,67},{67,3},{4,68},{68... | collective-permute-start | bytes 2359304 | tf_op jit(solution)/shard_map/ppermute | solution.py:509
  231.6 27.2 %copy-start.6 = (bf16[2,768,512]{2,1,0:T(8,128)(2,1)S(1)}, bf16[2,768,512]{2,1,0:T(8,128)(2,1)}, u32[]{:S(2)}) copy-start(bf16[2,768,512]{2,1,0:T(8,128)(2,1)} %copy-done.4) | copy-start | bytes 4718596
  231.7 1.3 collective-permute-start.13
  233.8 30.9 %all-to-all-start.6 = ((f32[64,16,128]{2,1,0:T(8,128)}), f32[64,16,128]{2,1,0:T(8,128)}, u32[]{:S(2)}, u32[]{:S(2)}) async-start(f32[64,16,128]{2,1,0:T(8,128)} %broadcast_in_dim.26), calls=%async_computation.6 | async-start | bytes 1048576 | tf_op jit(solution)/shard_map/all_to_all | solution.py:531
  262.5 5.2 %collective-permute-start.12 = (bf16[768,512]{1,0:T(8,128)(2,1)}, bf16[768,512]{1,0:T(8,128)(2,1)S(1)}, u32[]{:S(2)}, u32[]{:S(2)}) collective-permute-start(bf16[768,512]{1,0:T(8,128)(2,1)} %get-tuple-element.59), channel_id=1, source_target_pairs={{0,32},{32,0},{1,33},{33,1},{2,34},{34,2},{3,35},{35,3},{4,36},{36... | collective-permute-start | bytes 2359304 | tf_op jit(solution)/shard_map/ppermute | solution.py:455
  (53 other events, 260.1 us)
where the time goes:
time: 273 us; the launch traced here: 270 us
  waiting for transfers between devices  78.9 us (29%)
  blocking collectives  53.8 us (20%)
  local copies, waits for them, and re-layouts  45 us (16%)
  Pallas kernels  36.9 us (14%)
  starting transfers between devices  34.9 us (13%)
  other arithmetic  19.7 us (7%)
    all_to_all x4, waiting for transfers between devices, exchanged(): lax.all_to_all(rows, 'expert', split_axis=0, concat_axis=0, tiled=True)  57.4 us
    all_to_all x2, blocking collectives, exchanged(): lax.all_to_all(rows, 'expert', split_axis=0, concat_axis=0, tiled=True)  53.8 us
    unnamed x134, local copies, waits for them, and re-layouts  37.9 us
    all_to_all x4, starting transfers between devices, exchanged(): lax.all_to_all(rows, 'expert', split_axis=0, concat_axis=0, tiled=True)  22.5 us
    ppermute x2, waiting for transfers between devices, over_groups(): got = lax.ppermute(far, 'dp', [(0, 1), (1, 0)])  18.1 us
    select_n x8, other arithmetic, both(): return (jnp.where(first, own, other), jnp.where(first, other, own))  12.7 us
    pallas_call x4, Pallas kernels, run(): pl.pallas_call(kernel, out_shape=out_shape, in_specs=[pl.BlockSpec(memory...  10.8 us
    pallas_call x4, Pallas kernels, weight_blocks(): pl.pallas_call(kernel, grid=(2,), out_shape=out_shape, in_specs=[pl.Block...  8.85 us
  transfers between devices with their start and end apart: 19, of which 8 were waited for; matrix products, arithmetic and copies ran while one was open for 10% of the time, Pallas kernels for 7%

commit v1 on v0

v1 whole, which is shorter than its diff:
```python
import functools

import jax
import jax.numpy as jnp
import numpy as np
from jax import lax
from jax.experimental import pallas as pl
from jax.experimental.pallas import tpu as pltpu
from jax.sharding import PartitionSpec as P

EPS = 1e-05
BF = jnp.bfloat16
F32 = jnp.float32

ROWS = 32
CAP = 10
HALF = 2
TOK = ROWS * HALF
EXP = 32
USED = CAP * HALF
SLOT = 24
ALL = EXP * SLOT
LANE = 128


class Tables:
    def __init__(self, n, slots=SLOT):
        self.n, self.slots, self.rows, self.made = n, slots, n * slots, {}

    def get(self, name, make):
        if name not in self.made:
            self.made[name] = make()
        return self.made[name]

    def place_of(self, shape, axis):
        s = lax.broadcasted_iota(jnp.int32, shape, axis).astype(F32)
        expert = jnp.floor((s + 0.5) * (1.0 / self.slots))
        return expert, s - self.slots * expert

    def flags(self, test):
        return jnp.where(test, 1.0, 0.0)

    @property
    def expand(self):
        def make():
            shape = (self.n, self.rows)
            expert, slot = self.place_of(shape, 1)
            return self.flags(expert == lax.broadcasted_iota(jnp.int32, shape, 0).astype(F32))

        return self.get("expand", make)

    @property
    def expand_t(self):
        def make():
            shape = (self.rows, self.n)
            expert, slot = self.place_of(shape, 0)
            return self.flags(expert == lax.broadcasted_iota(jnp.int32, shape, 1).astype(F32))

        return self.get("expand_t", make)

    @property
    def slot_row(self):
        return self.get("slot_row", lambda: self.place_of((1, self.rows), 1)[1])

    @property
    def slot_column(self):
        return self.get("slot_column", lambda: self.place_of((self.rows, 1), 0)[1])

    @property
    def place(self):
        def make():
            shape = (self.rows, LANE)
            slot = self.place_of(shape, 0)[1]
            lane = lax.broadcasted_iota(jnp.int32, shape, 1).astype(F32)
            return self.flags((slot == lane) & (slot < USED))

        return self.get("place", make)

    def extra(self, i):
        return self.get(("extra", i), lambda: jnp.where(self.slot_row == USED + i, self.expand, 0.0).astype(BF))

    def extra_t(self, i):
        return self.get(("extra_t", i), lambda: jnp.where(self.slot_column == USED + i, self.expand_t, 0.0).astype(BF))


def dot(a, b):
    return lax.dot_general(a, b, (((1,), (0,)), ((), ())), preferred_element_type=F32)


def dot_t0(a, b):
    return lax.dot_general(a, b, (((0,), (0,)), ((), ())), preferred_element_type=F32)


def dot_t1(a, b):
    return lax.dot_general(a, b, (((1,), (1,)), ((), ())), preferred_element_type=F32)


def split2(v):
    hi = v.astype(BF)
    return hi, (v - hi.astype(F32)).astype(BF)


def split3(v):
    hi = v.astype(BF)
    rest = v - hi.astype(F32)
    mid = rest.astype(BF)
    return hi, mid, (rest - mid.astype(F32)).astype(BF)


def slots_of(picks, c, shift=0.0):
    columns = lax.broadcasted_iota(jnp.int32, (TOK, EXP), 1)
    mask = jnp.zeros((TOK, EXP), F32)
    for k in range(picks.shape[1]):
        mask = mask + jnp.where(picks[:, k : k + 1] == columns, 1.0, 0.0)
    row = lax.broadcasted_iota(jnp.int32, (TOK, TOK), 0)
    column = lax.broadcasted_iota(jnp.int32, (TOK, TOK), 1)
    earlier = jnp.where((column < row) & ((row < ROWS) | (column >= ROWS)), 1.0, 0.0).astype(BF)
    start = jnp.where(lax.broadcasted_iota(jnp.int32, (TOK, EXP), 0) < ROWS, 0.0, 1.0 * CAP)
    slot = mask * (dot(earlier, mask.astype(BF)) + start + 1.0 + shift) - 1.0
    table = dot(slot.astype(BF), c.expand.astype(BF)) == c.slot_row
    return mask, table


def one(table):
    return jnp.where(table, 1.0, 0.0).astype(BF)


def norm(tokens, gain):
    values = tokens.astype(F32)
    scale = lax.rsqrt(jnp.mean(values * values, axis=-1, keepdims=True) + EPS)
    return (values * scale * gain).astype(BF), scale, values


def mix(normed, router, mask):
    logits = dot_t1(normed, router)
    expo = jnp.where(mask > 0.0, jnp.exp(jnp.where(mask > 0.0, logits, 0.0)), 0.0)
    return expo / jnp.sum(expo, axis=-1, keepdims=True)


def weighted(table, parts, c):
    return [jnp.where(table, dot(v, c.expand.astype(BF)), 0.0) for v in parts]


def small_rows(masked, c):
    row = jnp.sum(masked, axis=0, keepdims=True)
    return dot((c.expand * row).astype(BF), c.place.astype(BF))


def small_columns(column, c):
    return dot(c.expand.astype(BF), (column.astype(F32) * c.place).astype(BF))


def spread_rows(smalls, c):
    total = None
    for i, v in enumerate(smalls):
        part = dot(c.extra_t(i), v.astype(BF))
        total = part if total is None else total + part
    return total


def column_of(first, index, c):
    wide = dot(c.expand_t.astype(BF), dot(c.extra(index), first).astype(BF))
    return jnp.sum(wide * c.place, axis=1, keepdims=True)


def with_small(rows, smalls, c):
    first = (rows[:, :LANE] + spread_rows(smalls, c)).astype(BF)
    return first, rows[:, LANE:].astype(BF)


def cost(flops, arrays):
    size = sum(int(np.prod(a.shape)) * jnp.dtype(a.dtype).itemsize for a in arrays)
    return pl.CostEstimate(flops=flops, bytes_accessed=size, transcendentals=0)


def call(kernel, name, outs, args, flops, at=None, scratch=(), grant=24):
    out_shape = [jax.ShapeDtypeStruct(s, d) for s, d in outs]
    scalars = [] if at is None else [at]
    return pl.pallas_call(
        kernel,
        out_shape=out_shape,
        in_specs=[pl.BlockSpec(memory_space=pltpu.SMEM)] * len(scalars)
        + [pl.BlockSpec(memory_space=pltpu.VMEM)] * len(args),
        out_specs=[pl.BlockSpec(memory_space=pltpu.VMEM)] * len(outs),
        scratch_shapes=list(scratch),
        name=name,
        cost_estimate=cost(flops, list(args) + out_shape),
        compiler_params=pltpu.CompilerParams(vmem_limit_bytes=grant << 20),
    )(*scalars, *args)


PART = 16
STEP = PART * SLOT


def each_part(body):
    @pl.loop(0, EXP // PART)
    def _(i):
        body(pl.ds(pl.multiple_of(i * STEP, STEP), STEP))


def start_kernel(at, inputs, cotangent, picks0, picks1, gain_own, gain_other, router_own, router_other, *outs):
    send, weights, tokens, grad, gains, routers = outs
    mine = at[0] == 0
    rows = pl.ds(pl.multiple_of(at[0] * TOK, TOK), TOK)
    own, other = gain_own[...], gain_other[...]
    gain0 = jnp.where(mine, own, other)
    gains[0:1, :] = gain0
    gains[1:2, :] = jnp.where(mine, other, own)
    own, other = router_own[...], router_other[...]
    router0 = jnp.where(mine, own, other)
    routers[0] = router0
    routers[1] = jnp.where(mine, other, own)
    token, cot = inputs[rows, :], cotangent[rows, :]
    tokens[...] = token
    grad[...] = cot
    c = Tables(EXP, 2 * SLOT)
    mask, table0 = slots_of(picks0[...], c)
    table1 = slots_of(picks1[...], c, 1.0 * SLOT)[1]
    normed, scale, values = norm(token, gain0)
    weights[...] = mix(normed, router0, mask)
    both = jnp.concatenate([one(table0), one(table1)], axis=0)
    send[...] = dot_t0(both, jnp.concatenate([normed, cot], axis=0)).astype(BF)


def halves_of(x, first, out):
    @pl.loop(0, EXP)
    def _(e):
        source = pl.multiple_of(e * 2 * SLOT + first, 8)
        out[pl.ds(pl.multiple_of(e * SLOT, 8), SLOT), :] = x[pl.ds(source, SLOT), :]


def forward0_kernel(x, wg, wu, wd, out, rows_out, fa, fb, hid):
    halves_of(x, 0, rows_out)

    def part(at):
        gate = dot(rows_out[at, :], wg[...])
        up = dot(rows_out[at, :], wu[...])
        sig = jax.nn.sigmoid(gate)
        act = gate * sig
        hidden = (act * up).astype(BF)
        hid[at, :] = hidden
        fb[at, :] = act
        fa[at, :] = up * sig * (1.0 + gate * (1.0 - sig))
        out[at, :] = dot(hidden, wd[...]).astype(BF)

    each_part(part)


def cotangent_kernel(x, out):
    halves_of(x, SLOT, out)


def expert1_kernel(x, g, wg, wu, wd, send, scaled_out, gate_out, up_out, hid):
    def part(at):
        c = Tables(PART)
        first = x[at, :LANE]
        weight = column_of(first, 0, c) + column_of(first, 1, c)
        gate = dot(x[at, :], wg[...])
        up = dot(x[at, :], wu[...])
        sig = jax.nn.sigmoid(gate)
        act = gate * sig
        hidden = (act * up).astype(BF)
        hid[at, :] = hidden
        out = dot(hidden, wd[...]).astype(BF)
        grad = g[at, :].astype(F32)
        weight_grad = jnp.sum(grad * out.astype(F32), axis=1, keepdims=True)
        scaled = (weight * grad).astype(BF)
        scaled_out[at, :] = scaled
        grad_hidden = dot_t1(scaled, wd[...])
        gate_back = (grad_hidden * (up * sig * (1.0 + gate * (1.0 - sig)))).astype(BF)
        up_back = (grad_hidden * act).astype(BF)
        gate_out[at, :] = gate_back
        up_out[at, :] = up_back
        back = dot_t1(gate_back, wg[...]) + dot_t1(up_back, wu[...])
        smalls = [small_columns(v, c) for v in split3(weight_grad)]
        send[at, :LANE], send[at, LANE:] = with_small(back, smalls, c)

    each_part(part)


def backward0_kernel(x, fa, fb, wd, gate_out, up_out):
    def part(at):
        grad_hidden = dot_t1(x[at, :], wd[...])
        gate_out[at, :] = (grad_hidden * fa[at, :]).astype(BF)
        up_out[at, :] = (grad_hidden * fb[at, :]).astype(BF)

    each_part(part)


def blocks_kernel(near, at, gb, ub, x, sc, hid, sent, kept):
    half, quarter = x.shape[1] // 2, x.shape[1] // 4
    group = at[1] if near else 1 - at[1]
    for which, out in ((1 - at[0], sent), (at[0], kept)):
        rows = x[:, pl.ds(pl.multiple_of(group * half + which * quarter, quarter), quarter)]
        out[0:quarter, :] = dot_t0(rows, gb[...]).astype(BF)
        out[quarter : 2 * quarter, :] = dot_t0(rows, ub[...]).astype(BF)
        low = hid[:, pl.ds(pl.multiple_of(which * quarter, quarter), quarter)]
        wide = sc[:, pl.ds(pl.multiple_of(group * half, half), half)]
        out[2 * quarter :, :] = dot_t0(low, wide).astype(BF)


def rest_kernel(at, x0, x1, x2, gb, ub, wg, wu, layer_gains, gains, out, total):
    total[...] = jnp.zeros_like(total)

    def part(at):
        c = Tables(PART)
        first = x2[at, :LANE]
        back = (dot_t1(gb[at, :], wg[...]) + dot_t1(ub[at, :], wu[...])).astype(BF).astype(F32)
        rows0 = x0[at, :].astype(F32)
        total[0:1, :] += jnp.sum(rows0 * column_of(first, 0, c), axis=0, keepdims=True)
        total[1:2, :] += jnp.sum(rows0 * back, axis=0, keepdims=True)
        total[2:3, :] += jnp.sum(x1[at, :].astype(F32) * column_of(first, 1, c), axis=0, keepdims=True)

    each_part(part)
    gain0 = total[1:2, :] / layer_gains[0:1, :] + gains[1:2, :]
    gain1 = gains[0:1, :]
    mine = at[0] == 0
    column0, column1 = total[0:1, :], total[2:3, :]
    out[0:1, :] = jnp.where(mine, column0, column1)
    out[1:2, :] = jnp.where(mine, gain0, gain1)
    out[2:3, :] = jnp.where(mine, column1, column0)
    out[3:4, :] = jnp.where(mine, gain1, gain0)


def finish_kernel(at, sum0, high0, low1, sum1, *outs):
    quarter = sum0.shape[0] // 3
    mine = at[0] == 0
    for i, out in enumerate(outs):
        rows = slice(i * quarter, (i + 1) * quarter)
        out[0:quarter, :] = jnp.where(mine, sum0[rows, :], low1[rows, :])
        out[quarter:, :] = jnp.where(mine, high0[rows, :], sum1[rows, :])


def middle_kernel(tokens, picks0, weights0, returned, picks1, gains, routers, mixed_out, send, weights1):
    c = Tables(EXP)
    mask0, table0 = slots_of(picks0[...], c)
    hi, lo = weighted(table0, split2(weights0[...]), c)
    back = returned[...]
    mixed = tokens[...].astype(F32) + dot(hi.astype(BF), back) + dot(lo.astype(BF), back)
    mixed = mixed.astype(BF)
    mixed_out[...] = mixed
    mask1, table1 = slots_of(picks1[...], c)
    normed, scale, values = norm(mixed, gains[1:2, :])
    weights = mix(normed, routers[1], mask1)
    weights1[...] = weights
    rows = dot_t0(one(table1), normed)
    smalls = [small_rows(v, c) for v in weighted(table1, split2(weights), c)]
    send[:, :LANE], send[:, LANE:] = with_small(rows, smalls, c)


def turn_kernel(tokens1, picks1, weights1, returned1, grad, tokens0, picks0, weights0, returned0, gains, routers, *outs):
    send, gains_out = outs
    c = Tables(EXP)
    gain0, gain1 = gains[0:1, :], gains[1:2, :]
    mask1, table1 = slots_of(picks1[...], c)
    back1 = returned1[...]
    pick1 = one(table1)
    expert_part = dot(pick1, back1)
    w1 = weights1[...]
    wg1 = jnp.zeros((TOK, EXP), F32)
    for i in range(3):
        column = column_of(back1[:, :LANE], i, c)
        wg1 = wg1 + dot(pick1, (column * c.expand_t).astype(BF))
    lg1 = (w1 * (wg1 - jnp.sum(w1 * wg1, axis=-1, keepdims=True))).astype(BF)
    normed1, scale1, values1 = norm(tokens1[...], gain1)
    normed_grad1 = dot(lg1, routers[1]) + expert_part
    gains_out[0:1, :] = jnp.sum(normed_grad1 * values1 * scale1, axis=0, keepdims=True)
    q = normed_grad1 * gain1
    grad_f = grad[...].astype(F32)
    g0 = (
        grad_f + scale1 * q - scale1 * scale1 * scale1 * values1 * jnp.mean(q * values1, axis=-1, keepdims=True)
    ).astype(BF)
    mask0, table0 = slots_of(picks0[...], c)
    w0 = weights0[...]
    met = jnp.where(table0, dot_t1(g0, returned0[...]), 0.0)
    wg0 = jnp.zeros((TOK, EXP), F32)
    for part in split3(met):
        wg0 = wg0 + dot(part, c.expand_t.astype(BF))
    lg0 = (w0 * (wg0 - jnp.sum(w0 * wg0, axis=-1, keepdims=True))).astype(BF)
    normed0, scale0, values0 = norm(tokens0[...], gain0)
    gains_out[1:2, :] = jnp.sum(dot(lg0, routers[0]) * values0 * scale0, axis=0, keepdims=True)
    hi, lo = weighted(table0, split2(w0), c)
    rows = dot_t0(hi.astype(BF), g0) + dot_t0(lo.astype(BF), g0)
    smalls = [small_rows(weighted(table0, [lg0], c)[0], c), small_rows(weighted(table1, [lg1], c)[0], c)]
    send[:, :LANE], send[:, LANE:] = with_small(rows, smalls, c)


def exchanged(rows):
    return lax.all_to_all(rows, "expert", split_axis=0, concat_axis=0, tiled=True)


def swapped(value):
    return lax.ppermute(value, "pipe", [(0, 1), (1, 0)])


def shards(inputs, cotangent, norm_gain, w_router, w_gate, w_up, w_down, routes):
    pipe = lax.axis_index("pipe")
    data = lax.axis_index("dp")
    at = jnp.stack([pipe, data]).astype(jnp.int32)
    width = inputs.shape[-1]
    inner = w_gate.shape[-1]
    half, quarter = width // 2, width // 4
    first = pipe == 0
    flops = ALL * width * inner

    def part_of(v, which):
        return lax.dynamic_slice_in_dim(v, which * HALF, HALF, 0).reshape(TOK, -1)

    def both(own, other):
        return jnp.where(first, own, other), jnp.where(first, other, own)

    picks0, picks1 = both(part_of(routes[0], pipe), swapped(part_of(routes[0], 1 - pipe)))
    router = w_router[0].T
    rows_shape = ((ALL, width), BF)
    inner_shape = ((ALL, inner), BF)
    few = ((TOK, width), BF)
    send0, weights0, tokens0, grad1, gains, routers = call(
        start_kernel,
        "start",
        [((2 * ALL, width), BF), ((TOK, EXP), F32), few, few, ((2, width), F32), ((2, EXP, width), BF)],
        [
            inputs.reshape(-1, width),
            cotangent.reshape(-1, width),
            picks0,
            picks1,
            norm_gain,
            swapped(norm_gain),
            router,
            swapped(router),
        ],
        400_000_000,
        at,
    )
    arrived = exchanged(send0)
    mats = [both(w[0, 0], swapped(w[0, 0])) for w in (w_gate, w_up, w_down)]
    (gate0, gate1), (up0, up1), (down0, down1) = lax.optimization_barrier(mats)

    out0, recv0, fa0, fb0, hidden0 = call(
        forward0_kernel,
        "forward0",
        [rows_shape, rows_shape, ((ALL, inner), F32), ((ALL, inner), F32), inner_shape],
        [arrived, gate0, up0, down0],
        6 * flops,
    )
    returned0 = exchanged(out0)
    (grad_rows,) = call(cotangent_kernel, "cotangent", [rows_shape], [arrived], 1000)

    tokens1, send1, weights1 = call(
        middle_kernel,
        "middle",
        [few, rows_shape, ((TOK, EXP), F32)],
        [tokens0, picks0, weights0, returned0, picks1, gains, routers],
        600_000_000,
    )
    recv1 = exchanged(send1)
    send_b, scaled1, gate_back1, up_back1, hidden1 = call(
        expert1_kernel,
        "expert1",
        [rows_shape, rows_shape, inner_shape, inner_shape, inner_shape],
        [recv1, grad_rows, gate1, up1, down1],
        12 * flops,
    )
    returned1 = exchanged(send_b)

    block = ((3 * quarter, half), BF)

    def blocks(near, args, name):
        return call(functools.partial(blocks_kernel, near), name, [block, block], args, 3 * flops, at)

    def far_part(args, name):
        sent, kept = blocks(False, args, name)
        paired = (kept.astype(F32) + swapped(sent).astype(F32)).astype(BF)
        return lax.ppermute(paired, "dp", [(0, 1), (1, 0)])

    def near_part(got, args, name):
        sent, kept = blocks(True, args, name)
        return (kept.astype(F32) + swapped(sent).astype(F32) + got.astype(F32)).astype(BF)

    args1 = [gate_back1, up_back1, recv1, scaled1, hidden1]
    sum1 = near_part(far_part(args1, "far1"), args1, "near1")
    low1 = lax.ppermute(sum1, "pipe", [(0, 1)])

    send2, token_gains = call(
        turn_kernel,
        "turn",
        [rows_shape, ((2, width), F32)],
        [tokens1, picks1, weights1, returned1, grad1, tokens0, picks0, weights0, returned0, gains, routers],
        900_000_000,
    )
    recv2 = exchanged(send2)
    gate_back0, up_back0 = call(
        backward0_kernel, "backward0", [inner_shape, inner_shape], [recv2, fa0, fb0, down0], 2 * flops
    )
    args0 = [gate_back0, up_back0, recv0, recv2, hidden0]
    got0 = far_part(args0, "far0")
    (small,) = call(
        rest_kernel,
        "rest",
        [((4, width), F32)],
        [recv0, recv1, recv2, gate_back0, up_back0, gate0, up0, gains, token_gains],
        4 * flops,
        at,
        [pltpu.VMEM((8, width), F32)],
    )
    mine = small[0:2] + swapped(small[2:4])
    group = 2 * EXP
    told = jnp.broadcast_to(mine.reshape(1, 2 * width // LANE, LANE), (group, 2 * width // LANE, LANE))
    heard = lax.all_to_all(told, ("dp", "expert"), split_axis=0, concat_axis=0, tiled=True)
    heard = heard.reshape(2, EXP, 2, width)
    router_sum = (heard[0, :, 0] + heard[1, :, 0]).T
    gain_sum = jnp.sum(heard[:, :, 1], axis=(0, 1))

    small, hidden0 = lax.optimization_barrier((small, hidden0))
    sum0 = near_part(got0, args0[:4] + [hidden0], "near0")
    high0 = lax.ppermute(sum0, "pipe", [(1, 0)])
    final = ((2 * quarter, half), BF)
    outs = call(finish_kernel, "finish", [final] * 3, [sum0, high0, low1, sum1], 1000, at)
    return (
        outs[0][None, None],
        outs[1][None, None],
        outs[2][None, None],
        router_sum[None],
        gain_sum[None],
    )


def solution(mesh):
    in_specs = (
        P(None, ("dp", "expert"), None),
        P(None, ("dp", "expert"), None),
        P("pipe", None),
        P("pipe", None, None),
        P("pipe", "expert", None, None),
        P("pipe", "expert", None, None),
        P("pipe", "expert", None, None),
        P("pipe", None, ("dp", "expert"), None),
    )
    out_specs = (
        P("pipe", "expert", "dp", None),
        P("pipe", "expert", "dp", None),
        P("pipe", "expert", None, "dp"),
        P("pipe", None, None),
        P("pipe", None),
    )
    return jax.shard_map(shards, mesh=mesh, in_specs=in_specs, out_specs=out_specs, check_vma=False)
```

time: 273 us -> 276 us (1.011)
  waiting for transfers between devices: 78.9 us -> 92.2 us
  other arithmetic: 19.7 us -> 13.4 us
  local copies, waits for them, and re-layouts: 45 us -> 40.7 us
  blocking collectives: 53.8 us -> 57.6 us
    all_to_all x4 -> x3, waiting for transfers between devices: 57.4 us -> 67.7 us  [exchanged(): lax.all_to_all(rows, 'expert', split_axis=0, concat_axis=0, tiled=True)]
    select_n x8 -> x4, other arithmetic: 12.7 us -> 5.61 us  [both(): return (jnp.where(first, own, other), jnp.where(first, other, own))]
    all_to_all x4 -> x3, starting transfers between devices: 22.5 us -> 17.3 us  [exchanged(): lax.all_to_all(rows, 'expert', split_axis=0, concat_axis=0, tiled=True)]
    all_to_all x2, blocking collectives: 53.8 us -> 57.6 us  [exchanged(): lax.all_to_all(rows, 'expert', split_axis=0, concat_axis=0, tiled=True)]
    squeeze x4 -> x0, local copies, waits for them, and re-layouts: 3.03 us -> none  [the longest x2 1.94 us: over_groups(): near = near[1].astype(F32) + swapped(near[0]).astype(F32)]
    ppermute x2 -> x4, starting transfers between devices: 3.52 us -> 6.23 us  [the longest x2 3.6 us: far_part(): return lax.ppermute(paired, 'dp', [(0, 1), (1, 0)])]
    unnamed x134 -> x123, local copies, waits for them, and re-layouts: 37.9 us -> 36.9 us
    ppermute x2 -> x4, waiting for transfers between devices: 18.1 us -> 18.6 us  [the longest x2 18.6 us: far_part(): return lax.ppermute(paired, 'dp', [(0, 1), (1, 0)])]
  transfers between devices with their start and end apart: 19 -> 19, of which waited for: 8 -> 9; matrix products, arithmetic and copies ran while one was open for 10% -> 7% of each run, Pallas kernels for 7% -> 5%
where the time goes in v1:
time: 276 us; the launch traced here: 274 us
  waiting for transfers between devices  92.2 us (33%)
  blocking collectives  57.6 us (21%)
  local copies, waits for them, and re-layouts  40.7 us (15%)
  Pallas kernels  35.8 us (13%)
  starting transfers between devices  32.8 us (12%)
  other arithmetic  13.4 us (5%)
    all_to_all x3, waiting for transfers between devices, exchanged(): lax.all_to_all(rows, 'expert', split_axis=0, concat_axis=0, tiled=True)  67.7 us
    all_to_all x2, blocking collectives, exchanged(): lax.all_to_all(rows, 'expert', split_axis=0, concat_axis=0, tiled=True)  57.6 us
    unnamed x123, local copies, waits for them, and re-layouts  36.9 us
    pallas_call x13, Pallas kernels, call(): pl.pallas_call(kernel, out_shape=out_shape, in_specs=[pl.BlockSpec(memory...  35.8 us
    ppermute x2, waiting for transfers between devices, far_part(): return lax.ppermute(paired, 'dp', [(0, 1), (1, 0)])  18.6 us
    all_to_all x3, starting transfers between devices, exchanged(): lax.all_to_all(rows, 'expert', split_axis=0, concat_axis=0, tiled=True)  17.3 us
    all_to_all x1, starting transfers between devices, shards(): lax.all_to_all(told, ('dp', 'expert'), split_axis=0, concat_axis=0, tiled...  6.94 us
    select_n x4, other arithmetic, both(): return (jnp.where(first, own, other), jnp.where(first, other, own))  5.61 us
  transfers between devices with their start and end apart: 19, of which 9 were waited for; matrix products, arithmetic and copies ran while one was open for 7% of the time, Pallas kernels for 5%

profile of v1, /device:TPU:0, one launch (start us, length us, event | category | flops | bytes accessed | tf_op | source)
XLA Modules:
  0.0 273.7 jit_solution(9413508593960356169)
XLA Ops:
  7.0 2.2 start.1
  9.2 1.6 copy-done.13
  11.4 9.4 %all-to-all-start = ((bf16[32,48,1024]{2,1,0:T(8,128)(2,1)}), bf16[32,48,1024]{2,1,0:T(8,128)(2,1)S(1)}, u32[]{:S(2)}, u32[]{:S(2)}) async-start(bf16[32,48,1024]{2,1,0:T(8,128)(2,1)} %bitcast.54), calls=%async_computation | async-start | bytes 6291456 | tf_op jit(solution)/shard_map/all_to_all | solution.py:390
  21.5 2.3 collective-permute-done.5
  23.7 2.7 broadcast_select_fusion
  29.5 34.8 %all-to-all-done = bf16[32,48,1024]{2,1,0:T(8,128)(2,1)S(1)} async-done(((bf16[32,48,1024]{2,1,0:T(8,128)(2,1)}), bf16[32,48,1024]{2,1,0:T(8,128)(2,1)S(1)}, u32[]{:S(2)}, u32[]{:S(2)}) %all-to-all-start) | async-done | bytes 3145760 | tf_op jit(solution)/shard_map/all_to_all | solution.py:390
  64.3 2.0 copy-done.7
  68.7 3.3 %forward0.1 = (bf16[768,1024]{1,0:T(8,128)(2,1)S(1)}, bf16[768,1024]{1,0:T(8,128)(2,1)S(1)}, f32[768,512]{1,0:T(8,128)S(1)}, f32[768,512]{1,0:T(8,128)S(1)}, bf16[768,512]{1,0:T(8,128)(2,1)S(1)}) custom-call(bf16[1536,1024]{1,0:T(8,128)(2,1)S(1)} %bitcast.49, bf16[1024,512]{1,0:T(8,128)(2,1)S(1)} %copy-done.9, bf16[1024,512]{1,0:T(8,128)(2,1)S(1)} %copy-done.7, ...), custom_call_target="tpu_custom_call" | custom-call | flops 2415919104 | bytes 13369344 | tf_op jit(solution)/shard_map/forward0/pallas_call | solution.py:179
  74.4 30.8 %all_to_all.60 = bf16[32,24,1024]{2,1,0:T(8,128)(2,1)S(1)} all-to-all(bf16[32,24,1024]{2,1,0:T(8,128)(2,1)S(1)} %bitcast.58), channel_id=1, replica_groups=mesh['dp'=2,'pipe'=2,'expert'=32] {'expert'}, dimensions={0} | all-to-all | bytes 3145728 | tf_op jit(solution)/shard_map/all_to_all | solution.py:390
  105.3 2.5 middle.1
  110.2 4.0 %all-to-all-start.2 = ((bf16[32,24,1024]{2,1,0:T(8,128)(2,1)}), bf16[32,24,1024]{2,1,0:T(8,128)(2,1)S(1)}, u32[]{:S(2)}, u32[]{:S(2)}) async-start(bf16[32,24,1024]{2,1,0:T(8,128)(2,1)} %bitcast.56), calls=%async_computation.2 | async-start | bytes 3145728 | tf_op jit(solution)/shard_map/all_to_all | solution.py:390
  114.2 1.9 copy-done.3
  117.5 19.1 %all-to-all-done.2 = bf16[32,24,1024]{2,1,0:T(8,128)(2,1)S(1)} async-done(((bf16[32,24,1024]{2,1,0:T(8,128)(2,1)}), bf16[32,24,1024]{2,1,0:T(8,128)(2,1)S(1)}, u32[]{:S(2)}, u32[]{:S(2)}) %all-to-all-start.2) | async-done | bytes 1572896 | tf_op jit(solution)/shard_map/all_to_all | solution.py:390
  141.7 7.0 %expert1.1 = (bf16[768,1024]{1,0:T(8,128)(2,1)S(1)}, bf16[768,1024]{1,0:T(8,128)(2,1)S(1)}, bf16[768,512]{1,0:T(8,128)(2,1)S(1)}, bf16[768,512]{1,0:T(8,128)(2,1)S(1)}, bf16[768,512]{1,0:T(8,128)(2,1)S(1)}) custom-call(bf16[768,1024]{1,0:T(8,128)(2,1)S(1)} %bitcast.45, bf16[768,1024]{1,0:T(8,128)(2,1)S(1)} %copy-done.32, bf16[1024,512]{1,0:T(8,128)(2,1)S(1)} %copy-done.35, ...), custom_call_target="tpu_custom_call" | custom-call | flops 4831838208 | bytes 11796480 | tf_op jit(solution)/shard_map/expert1/pallas_call | solution.py:179
  149.9 26.8 %all_to_all.61 = bf16[32,24,1024]{2,1,0:T(8,128)(2,1)S(1)} all-to-all(bf16[32,24,1024]{2,1,0:T(8,128)(2,1)S(1)} %bitcast.57), channel_id=1, replica_groups=mesh['dp'=2,'pipe'=2,'expert'=32] {'expert'}, dimensions={0} | all-to-all | bytes 3145728 | tf_op jit(solution)/shard_map/all_to_all | solution.py:390
  176.7 5.0 %turn.1 = (bf16[768,1024]{1,0:T(8,128)(2,1)S(1)}, f32[2,1024]{1,0:T(2,128)S(1)}) custom-call(bf16[64,1024]{1,0:T(8,128)(2,1)S(1)} %copy-done.41, s32[64,8]{1,0:T(8,128)S(1)} %copy-done.44, f32[64,32]{1,0:T(8,128)S(1)} %copy-done.52, bf16[768,1024]{1,0:T(8,128)(2,1)S(1)} %bitcast.53, bf16[64,1024]{1,0:T(8,128)(2,1)S(1)} %get-tuple-element.62.grad, ...), custom_call_target="tpu_custom_call" | custom-call | flops 900000000 | bytes 5279744 | tf_op jit(solution)/shard_map/turn/pallas_call | solution.py:179
  183.5 4.0 %all-to-all-start.4 = ((bf16[32,24,1024]{2,1,0:T(8,128)(2,1)}), bf16[32,24,1024]{2,1,0:T(8,128)(2,1)S(1)}, u32[]{:S(2)}, u32[]{:S(2)}) async-start(bf16[32,24,1024]{2,1,0:T(8,128)(2,1)} %bitcast.55), calls=%async_computation.4 | async-start | bytes 3145728 | tf_op jit(solution)/shard_map/all_to_all | solution.py:390
  192.3 2.7 far1.1
  195.9 13.9 %all-to-all-done.4 = bf16[32,24,1024]{2,1,0:T(8,128)(2,1)S(1)} async-done(((bf16[32,24,1024]{2,1,0:T(8,128)(2,1)}), bf16[32,24,1024]{2,1,0:T(8,128)(2,1)S(1)}, u32[]{:S(2)}, u32[]{:S(2)}) %all-to-all-start.4) | async-done | bytes 1572896 | tf_op jit(solution)/shard_map/all_to_all | solution.py:390
  215.4 2.0 far0.1
  217.5 2.0 near1.1
  221.6 2.8 %collective-permute-start.12 = (bf16[768,512]{1,0:T(8,128)(2,1)S(1)}, bf16[768,512]{1,0:T(8,128)(2,1)S(1)}, u32[]{:S(2)}, u32[]{:S(2)}) collective-permute-start(bf16[768,512]{1,0:T(8,128)(2,1)S(1)} %add_convert_fusion.1), channel_id=1, source_target_pairs={{0,64},{64,0},{1,65},{65,1},{2,66},{66,2},{3,67},{67,3},{4,68},{68... | collective-permute-start | bytes 2359304 | tf_op jit(solution)/shard_map/ppermute | solution.py:474
  224.4 3.8 %rest.1 = f32[4,1024]{1,0:T(4,128)S(1)} custom-call(s32[2]{0:T(128)S(1)} %pad_add_fusion.at, bf16[768,1024]{1,0:T(8,128)(2,1)S(1)} %copy-done.1, bf16[768,1024]{1,0:T(8,128)(2,1)S(1)} %bitcast.48, bf16[768,1024]{1,0:T(8,128)(2,1)S(1)} %bitcast.43, bf16[768,512]{1,0:T(8,128)(2,1)S(1)} %get-tuple-element.66.gb, bf16[768,512]{1,0:T(8,128)(2,1)S(1)} %get-tuple-element.67.ub, ...), custom_call_target="tpu_custom_call" | custom-call | flops 1610612736 | bytes 8421376 | tf_op jit(solution)/shard_map/rest/pallas_call | solution.py:179
  228.2 2.0 near0.1
  232.4 11.2 %collective-permute-done.12 = bf16[768,512]{1,0:T(8,128)(2,1)S(1)} collective-permute-done((bf16[768,512]{1,0:T(8,128)(2,1)S(1)}, bf16[768,512]{1,0:T(8,128)(2,1)S(1)}, u32[]{:S(2)}, u32[]{:S(2)}) %collective-permute-start.12) | collective-permute-done | bytes 786464 | tf_op jit(solution)/shard_map/ppermute | solution.py:474
  246.2 6.9 %all-to-all-start.5 = ((f32[64,16,128]{2,1,0:T(8,128)}), f32[64,16,128]{2,1,0:T(8,128)}, u32[]{:S(2)}, u32[]{:S(2)}) async-start(f32[64,16,128]{2,1,0:T(8,128)} %broadcast_in_dim.26), calls=%async_computation.5 | async-start | bytes 1048576 | tf_op jit(solution)/shard_map/all_to_all | solution.py:509
  253.1 7.5 %collective-permute-done.8 = bf16[768,512]{1,0:T(8,128)(2,1)} collective-permute-done((bf16[768,512]{1,0:T(8,128)(2,1)}, bf16[768,512]{1,0:T(8,128)(2,1)}, u32[]{:S(2)}, u32[]{:S(2)}) %collective-permute-start.8) | collective-permute-done | bytes 786464 | tf_op jit(solution)/shard_map/ppermute | solution.py:474
  260.6 1.7 add_convert_fusion.2.sum0
  263.6 2.4 all-to-all-done.5
  266.0 2.1 reshape.46
  270.0 1.9 slice_reduce_fusion
  271.9 1.8 finish.1
  (163 shorter events, 48.6 us)
Async XLA Ops:
  0.6 2.3 collective-permute-start.1
  1.5 1.4 collective-permute-start
  2.1 1.5 collective-permute-start.2
  11.4 52.9 %all-to-all-start = ((bf16[32,48,1024]{2,1,0:T(8,128)(2,1)}), bf16[32,48,1024]{2,1,0:T(8,128)(2,1)S(1)}, u32[]{:S(2)}, u32[]{:S(2)}) async-start(bf16[32,48,1024]{2,1,0:T(8,128)(2,1)} %bitcast.54), calls=%async_computation | async-start | bytes 6291456 | tf_op jit(solution)/shard_map/all_to_all | solution.py:390
  20.8 3.0 %collective-permute-start.5 = (bf16[512,1024]{1,0:T(8,128)(2,1)}, bf16[512,1024]{1,0:T(8,128)(2,1)S(1)}, u32[]{:S(2)}, u32[]{:S(2)}) collective-permute-start(bf16[512,1024]{1,0:T(8,128)(2,1)} %bitcast.63), channel_id=1, source_target_pairs={{0,32},{32,0},{1,33},{33,1},{2,34},{34,2},{3,35},{35,3},{4,36},{36... | collective-permute-start | bytes 3145736 | tf_op jit(solution)/shard_map/ppermute | solution.py:394
  20.9 5.5 %collective-permute-start.4 = (bf16[1024,512]{1,0:T(8,128)(2,1)}, bf16[1024,512]{1,0:T(8,128)(2,1)S(1)}, u32[]{:S(2)}, u32[]{:S(2)}) collective-permute-start(bf16[1024,512]{1,0:T(8,128)(2,1)} %bitcast.64), channel_id=1, source_target_pairs={{0,32},{32,0},{1,33},{33,1},{2,34},{34,2},{3,35},{35,3},{4,36},{36... | collective-permute-start | bytes 3145736 | tf_op jit(solution)/shard_map/ppermute | solution.py:394
  21.4 6.5 %collective-permute-start.3 = (bf16[1024,512]{1,0:T(8,128)(2,1)}, bf16[1024,512]{1,0:T(8,128)(2,1)S(1)}, u32[]{:S(2)}, u32[]{:S(2)}) collective-permute-start(bf16[1024,512]{1,0:T(8,128)(2,1)} %bitcast.65), channel_id=1, source_target_pairs={{0,32},{32,0},{1,33},{33,1},{2,34},{34,2},{3,35},{35,3},{4,36},{36... | collective-permute-start | bytes 3145736 | tf_op jit(solution)/shard_map/ppermute | solution.py:394
  74.4 30.9 %copy-start = (bf16[768,1024]{1,0:T(8,128)(2,1)}, bf16[768,1024]{1,0:T(8,128)(2,1)S(1)}, u32[]{:S(2)}) copy-start(bf16[768,1024]{1,0:T(8,128)(2,1)S(1)} %get-tuple-element.68.x0.x) | copy-start | bytes 4718596
  74.4 30.9 %copy-start.14 = (bf16[768,512]{1,0:T(8,128)(2,1)}, bf16[768,512]{1,0:T(8,128)(2,1)S(1)}, u32[]{:S(2)}) copy-start(bf16[768,512]{1,0:T(8,128)(2,1)S(1)} %get-tuple-element.71.hid) | copy-start | bytes 2359300
  74.4 30.9 %copy-start.43 = (s32[64,8]{1,0:T(8,128)S(1)}, s32[64,8]{1,0:T(8,128)}, u32[]{:S(2)}) copy-start(s32[64,8]{1,0:T(8,128)} %copy-done.42) | copy-start | bytes 6148
  74.4 30.9 %copy-start.46 = (s32[64,8]{1,0:T(8,128)S(1)}, s32[64,8]{1,0:T(8,128)}, u32[]{:S(2)}) copy-start(s32[64,8]{1,0:T(8,128)} %copy-done.45) | copy-start | bytes 6148
  74.4 30.9 %copy-start.49 = (f32[64,32]{1,0:T(8,128)S(1)}, f32[64,32]{1,0:T(8,128)}, u32[]{:S(2)}) copy-start(f32[64,32]{1,0:T(8,128)} %copy-done.48) | copy-start | bytes 24580
  110.2 26.3 %all-to-all-start.2 = ((bf16[32,24,1024]{2,1,0:T(8,128)(2,1)}), bf16[32,24,1024]{2,1,0:T(8,128)(2,1)S(1)}, u32[]{:S(2)}, u32[]{:S(2)}) async-start(bf16[32,24,1024]{2,1,0:T(8,128)(2,1)} %bitcast.56), calls=%async_computation.2 | async-start | bytes 3145728 | tf_op jit(solution)/shard_map/all_to_all | solution.py:390
  149.8 26.8 %copy-start.16 = (bf16[768,512]{1,0:T(8,128)(2,1)}, bf16[768,512]{1,0:T(8,128)(2,1)S(1)}, u32[]{:S(2)}) copy-start(bf16[768,512]{1,0:T(8,128)(2,1)S(1)} %get-tuple-element.76.gb) | copy-start | bytes 2359300
  149.8 26.8 %copy-start.19 = (bf16[768,512]{1,0:T(8,128)(2,1)}, bf16[768,512]{1,0:T(8,128)(2,1)S(1)}, u32[]{:S(2)}) copy-start(bf16[768,512]{1,0:T(8,128)(2,1)S(1)} %get-tuple-element.77.ub) | copy-start | bytes 2359300
  149.8 26.8 %copy-start.22 = (bf16[768,512]{1,0:T(8,128)(2,1)}, bf16[768,512]{1,0:T(8,128)(2,1)S(1)}, u32[]{:S(2)}) copy-start(bf16[768,512]{1,0:T(8,128)(2,1)S(1)} %get-tuple-element.79.hid) | copy-start | bytes 2359300
  149.8 26.8 %copy-start.41 = (bf16[64,1024]{1,0:T(8,128)(2,1)S(1)}, bf16[64,1024]{1,0:T(8,128)(2,1)}, u32[]{:S(2)}) copy-start(bf16[64,1024]{1,0:T(8,128)(2,1)} %copy-done.40) | copy-start | bytes 393220
  149.8 26.8 %copy-start.44 = (s32[64,8]{1,0:T(8,128)S(1)}, s32[64,8]{1,0:T(8,128)}, u32[]{:S(2)}) copy-start(s32[64,8]{1,0:T(8,128)} %copy-done.42) | copy-start | bytes 6148
  149.9 26.8 %copy-start.47 = (s32[64,8]{1,0:T(8,128)S(1)}, s32[64,8]{1,0:T(8,128)}, u32[]{:S(2)}) copy-start(s32[64,8]{1,0:T(8,128)} %copy-done.45) | copy-start | bytes 6148
  149.9 26.8 %copy-start.50 = (f32[64,32]{1,0:T(8,128)S(1)}, f32[64,32]{1,0:T(8,128)}, u32[]{:S(2)}) copy-start(f32[64,32]{1,0:T(8,128)} %copy-done.48) | copy-start | bytes 24580
  149.9 26.8 %copy-start.52 = (f32[64,32]{1,0:T(8,128)S(1)}, f32[64,32]{1,0:T(8,128)}, u32[]{:S(2)}) copy-start(f32[64,32]{1,0:T(8,128)} %copy-done.51) | copy-start | bytes 24580
  183.5 26.2 %all-to-all-start.4 = ((bf16[32,24,1024]{2,1,0:T(8,128)(2,1)}), bf16[32,24,1024]{2,1,0:T(8,128)(2,1)S(1)}, u32[]{:S(2)}, u32[]{:S(2)}) async-start(bf16[32,24,1024]{2,1,0:T(8,128)(2,1)} %bitcast.55), calls=%async_computation.4 | async-start | bytes 3145728 | tf_op jit(solution)/shard_map/all_to_all | solution.py:390
  195.9 24.2 %collective-permute-start.11 = (bf16[768,512]{1,0:T(8,128)(2,1)}, bf16[768,512]{1,0:T(8,128)(2,1)}, u32[]{:S(2)}, u32[]{:S(2)}) collective-permute-start(bf16[768,512]{1,0:T(8,128)(2,1)} %get-tuple-element.83), channel_id=1, source_target_pairs={{0,32},{32,0},{1,33},{33,1},{2,34},{34,2},{3,35},{35,3},{4,36},{36... | collective-permute-start | bytes 2359304 | tf_op jit(solution)/shard_map/ppermute | solution.py:394
  217.4 12.8 %collective-permute-start.7 = (bf16[768,512]{1,0:T(8,128)(2,1)S(1)}, bf16[768,512]{1,0:T(8,128)(2,1)S(1)}, u32[]{:S(2)}, u32[]{:S(2)}) collective-permute-start(bf16[768,512]{1,0:T(8,128)(2,1)S(1)} %get-tuple-element.75), channel_id=1, source_target_pairs={{0,32},{32,0},{1,33},{33,1},{2,34},{34,2},{3,35},{35,3},{4,36},{36... | collective-permute-start | bytes 2359304 | tf_op jit(solution)/shard_map/ppermute | solution.py:394
  219.6 12.8 %collective-permute-start.10 = (bf16[768,512]{1,0:T(8,128)(2,1)S(1)}, bf16[768,512]{1,0:T(8,128)(2,1)S(1)}, u32[]{:S(2)}, u32[]{:S(2)}) collective-permute-start(bf16[768,512]{1,0:T(8,128)(2,1)S(1)} %get-tuple-element.81), channel_id=1, source_target_pairs={{0,32},{32,0},{1,33},{33,1},{2,34},{34,2},{3,35},{35,3},{4,36},{36... | collective-permute-start | bytes 2359304 | tf_op jit(solution)/shard_map/ppermute | solution.py:394
  221.6 22.0 %collective-permute-start.12 = (bf16[768,512]{1,0:T(8,128)(2,1)S(1)}, bf16[768,512]{1,0:T(8,128)(2,1)S(1)}, u32[]{:S(2)}, u32[]{:S(2)}) collective-permute-start(bf16[768,512]{1,0:T(8,128)(2,1)S(1)} %add_convert_fusion.1), channel_id=1, source_target_pairs={{0,64},{64,0},{1,65},{65,1},{2,66},{66,2},{3,67},{67,3},{4,68},{68... | collective-permute-start | bytes 2359304 | tf_op jit(solution)/shard_map/ppermute | solution.py:474
  230.2 22.9 %collective-permute-start.6 = (bf16[768,512]{1,0:T(8,128)(2,1)S(1)}, bf16[768,512]{1,0:T(8,128)(2,1)}, u32[]{:S(2)}, u32[]{:S(2)}) collective-permute-start(bf16[768,512]{1,0:T(8,128)(2,1)S(1)} %get-tuple-element.73), channel_id=1, source_target_pairs={{0,32},{32,0},{1,33},{33,1},{2,34},{34,2},{3,35},{35,3},{4,36},{36... | collective-permute-start | bytes 2359304 | tf_op jit(solution)/shard_map/ppermute | solution.py:394
  231.4 29.2 %collective-permute-start.8 = (bf16[768,512]{1,0:T(8,128)(2,1)}, bf16[768,512]{1,0:T(8,128)(2,1)}, u32[]{:S(2)}, u32[]{:S(2)}) collective-permute-start(bf16[768,512]{1,0:T(8,128)(2,1)} %add_convert_fusion.3), channel_id=1, source_target_pairs={{0,64},{64,0},{1,65},{65,1},{2,66},{66,2},{3,67},{67,3},{4,68},{68... | collective-permute-start | bytes 2359304 | tf_op jit(solution)/shard_map/ppermute | solution.py:474
  232.2 13.1 %collective-permute-start.14 = (f32[2,1024]{1,0:T(2,128)S(1)}, f32[2,1024]{1,0:T(2,128)S(1)}, u32[]{:S(2)}, u32[]{:S(2)}) collective-permute-start(f32[2,1024]{1,0:T(2,128)S(1)} %slice.21), channel_id=1, source_target_pairs={{0,32},{32,0},{1,33},{33,1},{2,34},{34,2},{3,35},{35,3},{4,36},{36... | collective-permute-start | bytes 24584 | tf_op jit(solution)/shard_map/ppermute | solution.py:394
  243.9 28.0 %collective-permute-start.13 = (bf16[768,512]{1,0:T(8,128)(2,1)S(1)}, bf16[768,512]{1,0:T(8,128)(2,1)S(1)}, u32[]{:S(2)}, u32[]{:S(2)}) collective-permute-start(bf16[768,512]{1,0:T(8,128)(2,1)S(1)} %add_convert_fusion.sum1), channel_id=1, source_target_pairs={{0,32},{1,33},{2,34},{3,35},{4,36},{5,37},{6,38},{7,39},{8,40},{9,... | collective-permute-start | bytes 2359304 | tf_op jit(solution)/shard_map/ppermute | solution.py:482
  246.2 19.9 %all-to-all-start.5 = ((f32[64,16,128]{2,1,0:T(8,128)}), f32[64,16,128]{2,1,0:T(8,128)}, u32[]{:S(2)}, u32[]{:S(2)}) async-start(f32[64,16,128]{2,1,0:T(8,128)} %broadcast_in_dim.26), calls=%async_computation.5 | async-start | bytes 1048576 | tf_op jit(solution)/shard_map/all_to_all | solution.py:509
  262.3 9.6 %collective-permute-start.9 = (bf16[768,512]{1,0:T(8,128)(2,1)S(1)}, bf16[768,512]{1,0:T(8,128)(2,1)S(1)}, u32[]{:S(2)}, u32[]{:S(2)}) collective-permute-start(bf16[768,512]{1,0:T(8,128)(2,1)S(1)} %add_convert_fusion.2.sum0), channel_id=1, source_target_pairs={{32,0},{33,1},{34,2},{35,3},{36,4},{37,5},{38,6},{39,7},{40,8},{41... | collective-permute-start | bytes 2359304 | tf_op jit(solution)/shard_map/ppermute | solution.py:516
  (48 other events, 122.5 us)
